TPU v7x, 128 devices: a whole 4x4x4 slice. The times are simulated.
128 devices in a mesh: sky: 16 (over x, z), depth: 8 (over y, core).
Axes of the slice: x: 4, y: 4, z: 4, core: 2. Of those that a mesh axis runs over, the one named last changes fastest.
Arguments:
- positions: float32 [3, 2048, 128], P(None, ('sky', 'depth')), may hold values from 0 to 1
- cell_points: int32 [2048], P(('sky', 'depth')), may hold values from 1 to 128
- target_log: float32 [16], replicated, may hold values from 8 to 20
- export_count: int32 [128, 128], P(('sky', 'depth')), may hold values from 0 to 3, as said below
- export_cell: int32 [128, 128, 3], P(('sky', 'depth')), may hold values from 0 to 15
- import_pair: int32 [128, 128, 3], P(('sky', 'depth')), may hold values from 0 to 15
- import_shift: int32 [3, 128, 128, 3], P(None, ('sky', 'depth')), may hold values from -1 to 1, as said below
Outputs:
- travel: float32 [3, 2048, 128], P(None, ('sky', 'depth'))
Inputs may be any that keep to these rules, and one draw needn't show every extreme that they name: export_count[s, t] counts the slots of export_cell[s, t] that are used; it is zero unless s and t are distinct devices whose sky indices differ by at most one modulo the sky axis's size and whose depth indices differ by at most one; in every draw some device t receives 3 cells from each such neighbour. For neighbouring devices t and s, components 0 and 2 of import_shift[:, t, s, k] are the sky step and the depth step from t's region to s's region (sky taken around the cycle), component 1 varies; all components are zero for devices that are not neighbours.
All inputs are finite; a program needn't handle non-finite values.
Results may differ from a plain program's by a relative error of at most 0.00022.
Values sent between devices are 32-bit elements; how exact they have to be, the bound alone decides.
No kernel may reach another device: no remote copies, remote signals or barrier semaphores. Data moves between devices by JAX's collectives and lax.ppermute only.
A program may use at most 64 MiB of HBM per device.

v0:
```python
import jax
import jax.numpy as jnp
from jax import lax
from jax.sharding import PartitionSpec as P

STEPS = 2


EPS_SQ = 0.0001
INV_WIDTH = 16.0
STEP_SIZE = 0.01
ROW_BLOCK = 8


def from_behind(array, axis, by):
    size = lax.axis_size(axis)
    return lax.ppermute(array, axis, [(i, (i + by) % size) for i in range(size)])


def from_behind_2(value, axis, steps):
    count = lax.axis_size(axis)
    initial, last = (max(0, -steps), min(count, count - steps))
    return lax.ppermute(value, axis, [(source, source + steps) for source in range(initial, last)])


def pair_geometry(left_pos, left_mask, right_pos, right_mask, shifts, centres):
    offsets = left_pos[:, :, :, None] - right_pos[:, :, None, :] - shifts[:, :, None, None]
    radius = jnp.sqrt(jnp.sum(offsets * offsets, axis=0) + EPS_SQ)
    weight = left_mask[:, :, None] * right_mask[:, None, :]
    scaled = (radius[None] - centres[:, None, None, None]) * INV_WIDTH
    kernel = jnp.exp(-0.5 * scaled * scaled)
    return (offsets, radius, weight, scaled, kernel)


def block_counts(left_pos, left_mask, right_pos, right_mask, shifts, centres):
    offsets, radius, weight, scaled, kernel = pair_geometry(
        left_pos, left_mask, right_pos, right_mask, shifts, centres
    )
    return jnp.sum(weight[None] * kernel, axis=(1, 2, 3))


def block_forces(left_pos, left_mask, right_pos, right_mask, shifts, centres, bin_pull):
    offsets, radius, weight, scaled, kernel = pair_geometry(
        left_pos, left_mask, right_pos, right_mask, shifts, centres
    )
    slopes = jnp.sum(bin_pull[:, None, None, None] * scaled * kernel, axis=0) * -INV_WIDTH
    strength = weight * slopes / radius
    pulled = strength[None] * offsets
    return (jnp.sum(pulled, axis=3), -jnp.sum(pulled, axis=2))


def take_block(left_pos, left_mask, right_pos, right_mask, shifts, first_row):
    return (
        lax.dynamic_slice_in_dim(left_pos, first_row, ROW_BLOCK, 1),
        lax.dynamic_slice_in_dim(left_mask, first_row, ROW_BLOCK, 0),
        lax.dynamic_slice_in_dim(right_pos, first_row, ROW_BLOCK, 1),
        lax.dynamic_slice_in_dim(right_mask, first_row, ROW_BLOCK, 0),
        lax.dynamic_slice_in_dim(shifts, first_row, ROW_BLOCK, 1),
    )


def ghost_counts(left_pos, left_mask, right_pos, right_mask, shifts, centres):
    block_total = left_pos.shape[1] // ROW_BLOCK

    def add_block(block_id, running):
        pieces = take_block(
            left_pos, left_mask, right_pos, right_mask, shifts, block_id * ROW_BLOCK
        )
        return running + block_counts(
            pieces[0], pieces[1], pieces[2], pieces[3], pieces[4], centres
        )

    return lax.fori_loop(0, block_total, add_block, jnp.zeros(centres.shape, jnp.float32))


def ghost_forces(left_pos, left_mask, right_pos, right_mask, shifts, centres, bin_pull):
    block_total = left_pos.shape[1] // ROW_BLOCK

    def add_block(block_id, buffers):
        first_row = block_id * ROW_BLOCK
        pieces = take_block(left_pos, left_mask, right_pos, right_mask, shifts, first_row)
        force_left, force_right = block_forces(
            pieces[0], pieces[1], pieces[2], pieces[3], pieces[4], centres, bin_pull
        )
        return (
            lax.dynamic_update_slice_in_dim(buffers[0], force_left, first_row, 1),
            lax.dynamic_update_slice_in_dim(buffers[1], force_right, first_row, 1),
        )

    empty = jnp.zeros(left_pos.shape, jnp.float32)
    return lax.fori_loop(0, block_total, add_block, (empty, empty))


def region_offsets():
    return [
        (across, along)
        for across in (-1, 0, 1)
        for along in (-1, 0, 1)
        if (across, along) != (0, 0)
    ]


def neighbour_table():
    sky_here = lax.axis_index("sky")
    depth_here = lax.axis_index("depth")
    sky_count = lax.axis_size("sky")
    depth_count = lax.axis_size("depth")
    near_ids = []
    near_valid = []
    for across, along in region_offsets():
        depth_there = depth_here + along
        inside = (depth_there >= 0) & (depth_there < depth_count)
        clamped = jnp.clip(depth_there, 0, depth_count - 1)
        near_ids.append((sky_here + across) % sky_count * depth_count + clamped)
        near_valid.append(inside)
    return (jnp.stack(near_ids), jnp.stack(near_valid))


def near_sizes(sizes_near):
    received = [None] * 8
    for index, (across, along) in enumerate(region_offsets()):
        piece = sizes_near[index]
        if across != 0:
            piece = from_behind(piece, "sky", across)
        if along != 0:
            piece = from_behind_2(piece, "depth", along)
        received[7 - index] = piece
    return jnp.stack(received)


def near_cells(cells_near):
    received = [None] * 8
    for index, (across, along) in enumerate(region_offsets()):
        piece = cells_near[:, index]
        if across != 0:
            piece = from_behind(piece, "sky", across)
        if along != 0:
            piece = from_behind_2(piece, "depth", along)
        received[7 - index] = piece
    return jnp.stack(received, axis=1)


def near_forces(forces_near):
    received = [None] * 8
    for index, (across, along) in enumerate(region_offsets()):
        piece = forces_near[:, index]
        if across != 0:
            piece = from_behind(piece, "sky", across)
        if along != 0:
            piece = from_behind_2(piece, "depth", along)
        received[7 - index] = piece
    return jnp.stack(received, axis=1)


def send_sizes(sizes_out, near_ids, near_valid):
    return near_sizes(sizes_out[near_ids] * near_valid[:, None].astype(jnp.int32))


def send_cells(coords, export_row, near_ids):
    peer_count, slot_count = export_row.shape
    outgoing = coords[:, export_row[near_ids].reshape(-1)].reshape(
        3, 8, slot_count, coords.shape[2]
    )
    return near_cells(outgoing)


def send_forces(forces_near):
    return near_forces(forces_near)


def body(positions, cell_points, target_log, export_count, export_cell, import_pair, import_shift):
    cell_count = positions.shape[1]
    points = positions.shape[2]
    slot_count = export_cell.shape[2]
    ghosts = 8 * slot_count
    centres = (jnp.arange(target_log.shape[0], dtype=jnp.float32) + 0.5) / INV_WIDTH
    point_ids = jnp.arange(points, dtype=jnp.int32)
    point_mask = (point_ids[None, :] < cell_points[:, None]).astype(jnp.float32)
    cell_ids = jnp.arange(cell_count, dtype=jnp.int32)
    near_ids, near_valid = neighbour_table()
    live_out = jnp.arange(slot_count, dtype=jnp.int32)[None, :] < export_count[0][:, None]
    sizes_out = jnp.where(live_out, cell_points[export_cell[0]], 0)
    sizes_in = send_sizes(sizes_out, near_ids, near_valid)
    ghost_mask = (point_ids[None, :] < sizes_in.reshape(-1)[:, None]).astype(jnp.float32)
    cells_near = export_cell[0][near_ids].reshape(-1)
    live_near = (live_out[near_ids] & near_valid[:, None]).reshape(-1)
    pair_cells = import_pair[0][near_ids].reshape(-1)
    shifts = import_shift[:, 0][:, near_ids].reshape(3, ghosts).astype(jnp.float32)
    left_mask = point_mask[pair_cells]
    onehot_pair = (pair_cells[:, None] == cell_ids[None, :]).astype(jnp.float32)
    onehot_out = ((cells_near[:, None] == cell_ids[None, :]) & live_near[:, None]).astype(
        jnp.float32
    )
    zero_shift = jnp.zeros((3, cell_count), jnp.float32)
    valid_local = jnp.sum(point_mask)
    coords = positions
    travel = jnp.zeros_like(positions)
    for iteration in range(STEPS):
        ghost_pos = send_cells(coords, export_cell[0], near_ids).reshape(3, ghosts, points)
        left_pos = coords[:, pair_cells]
        self_total = block_counts(coords, point_mask, coords, point_mask, zero_shift, centres)
        ghost_total = ghost_counts(left_pos, left_mask, ghost_pos, ghost_mask, shifts, centres)
        counts = lax.psum(0.5 * self_total + ghost_total, ("sky", "depth"))
        mean_count = jnp.mean(counts)
        bin_pull = (jnp.log(1.0 + counts) - target_log) * mean_count / (1.0 + counts)
        self_grad, unused_right = block_forces(
            coords, point_mask, coords, point_mask, zero_shift, centres, bin_pull
        )
        force_left, force_right = ghost_forces(
            left_pos, left_mask, ghost_pos, ghost_mask, shifts, centres, bin_pull
        )
        returned = send_forces(force_right.reshape(3, 8, slot_count, points)).reshape(
            3, ghosts, points
        )
        gradient = self_grad
        gradient = gradient + jnp.einsum(
            "gc,kgp->kcp", onehot_pair, force_left, precision=lax.Precision.HIGHEST
        )
        gradient = gradient + jnp.einsum(
            "gc,kgp->kcp", onehot_out, returned, precision=lax.Precision.HIGHEST
        )
        power_sum, valid_count = lax.psum(
            (jnp.sum(gradient * gradient), valid_local), ("sky", "depth")
        )
        grad_rms = jnp.sqrt(power_sum / (3.0 * valid_count) + 1e-06)
        move_dir = -gradient / grad_rms
        travel = travel + move_dir
        coords = coords + STEP_SIZE * move_dir
    return travel


def solution(mesh):
    in_specs = (
        P(None, ("sky", "depth"), None),
        P(("sky", "depth")),
        P(),
        P(("sky", "depth"), None),
        P(("sky", "depth"), None, None),
        P(("sky", "depth"), None, None),
        P(None, ("sky", "depth"), None, None),
    )
    out_specs = P(None, ("sky", "depth"), None)
    return jax.shard_map(body, mesh=mesh, in_specs=in_specs, out_specs=out_specs, check_vma=False)
```

profile of v0, /device:TPU:1, one launch (start us, length us, event | category | flops | bytes accessed | tf_op | source)
XLA Modules:
  0.0 525.2 jit_solution(16160007866016866266)
XLA Ops:
  3.0 10.6 %fusion.60 = s32[128,3]{1,0:T(8,128)S(1)} fusion(s32[1,128,3]{2,1,0:T(8,128)S(1)} %copy.87, s32[]{:T(128)} %bitcast.31, s32[]{:T(128)} %bitcast.32, s32[]{:T(128)} %bitcast.33, s32[]{:T(128)} %bitcast.34, s32[]{:T(128)} %bitcast.35, s32[]{:T(128)} %bitcast.37, s32[]{:T(128)} %bitcast.36, s32[]{:T(128)} %bitcast.14, s32[]{:T(128)} %bitcast.16, s32[]{:T(128)} %bitcast.18, ...), kind=kLoop, calls=%fused_computation.175 | loop fusion | flops 13440 | bytes 3648 | tf_op jit(solution)/shard_map/jit(_where)/select_n | solution.py:182
  19.7 4.6 collective-permute-start.5
  31.1 5.1 fusion.36
  39.6 4.8 collective-permute-start.7
  47.4 5.0 collective-permute-start.17
  70.5 3.6 collective-permute-start.13
  74.9 3.4 collective-permute-start.19
  84.2 5.6 %collective-permute-start.20 = (f32[3,3,128]{2,1,0:T(4,128)S(1)}, f32[3,3,128]{2,1,0:T(4,128)S(1)}, u32[]{:S(2)}, u32[]{:S(2)}) collective-permute-start(f32[3,3,128]{2,1,0:T(4,128)S(1)} %collective-permute-done.19), channel_id=1, source_target_pairs={{0,1},{1,2},{2,3},{3,4},{4,5},{5,6},{6,7},{8,9},{9,10},{10,11},{11... | collective-permute-start | bytes 13832 | tf_op jit(solution)/shard_map/ppermute | solution.py:23
  94.8 10.7 %while.70 = (s32[]{:T(128)}, f32[16]{0:T(128)S(1)}, f32[24,128]{1,0:T(8,128)S(1)}, f32[24,128]{1,0:T(8,128)S(1)}, f32[3,24,128]{2,1,0:T(8,128)S(1)}, /*index=5*/...) while((s32[]{:T(128)}, f32[16]{0:T(128)S(1)}, ...), condition=%wide.region_5.6_spmd.clone, body=%wide.region_2.5_spmd.clone.sunk | while | flops 14286903 | bytes 3244889 | solution.py:73
  105.6 62.9 %psum.38 = f32[16]{0:T(128)S(1)} all-reduce(f32[16]{0:T(128)S(1)} %multiply_add_fusion.2), channel_id=1, replica_groups=mesh['sky'=16,'depth'=8] {'sky','depth'}, use_global_device_ids=true, to_apply=%region_6.7 | all-reduce | flops 16 | bytes 128 | tf_op jit(solution)/shard_map/psum | solution.py:203
  169.6 5.4 %fusion.37 = f32[16,128,128]{2,1,0:T(8,128)S(1)} fusion(f32[16]{0:T(128)S(1)} %get-tuple-element.1089, f32[16]{0:T(128)S(1)} %add_multiply_fusion.4, f32[16,128,128]{2,1,0:T(8,128)S(1)} %get-tuple-element.1163), kind=kLoop, calls=%fused_computation.105 | loop fusion | flops 29097984 | bytes 2097280 | tf_op jit(solution)/shard_map/reduce_sum | solution.py:46
  175.4 14.3 %while.68 = (s32[]{:T(128)}, f32[3,24,128]{2,1,0:T(8,128)S(1)}, f32[3,24,128]{2,1,0:T(8,128)S(1)}, f32[24,128]{1,0:T(8,128)S(1)}, f32[24,128]{1,0:T(8,128)S(1)},...) while((s32[]{:T(128)}, f32[3,24,128]{2,1,0:T(8,128)S(1)}, ...), condition=%wide.region_15.16_spmd.clone, body=%wide.region_10.0_spmd.clone.sunk | while | flops 18740276 | bytes 4916107 | solution.py:91
  199.4 3.6 collective-permute-start.25
  203.8 4.1 collective-permute-start.31
  210.2 3.7 collective-permute-start.33
  213.9 5.3 %collective-permute-start.32 = (f32[3,3,128]{2,1,0:T(4,128)S(1)}, f32[3,3,128]{2,1,0:T(4,128)S(1)}, u32[]{:S(2)}, u32[]{:S(2)}) collective-permute-start(f32[3,3,128]{2,1,0:T(4,128)S(1)} %collective-permute-done.31), channel_id=1, source_target_pairs={{0,1},{1,2},{2,3},{3,4},{4,5},{5,6},{6,7},{8,9},{9,10},{10,11},{11... | collective-permute-start | bytes 13832 | tf_op jit(solution)/shard_map/ppermute | solution.py:23
  225.0 62.3 %all-reduce = (f32[]{:T(128)}, f32[]{:T(128)}) all-reduce(f32[]{:T(128)} %get-tuple-element.1159, f32[]{:T(128)} %fusion.76), channel_id=1, replica_groups=mesh['sky'=16,'depth'=8] {'sky','depth'}, use_global_device_ids=true, to_apply=%region_17.18 | all-reduce | flops 2 | bytes 16 | tf_op jit(solution)/shard_map/psum | solution.py:222
  291.5 4.8 collective-permute-done.36
  296.3 4.4 collective-permute-start.37
  300.8 5.1 fusion.42
  311.0 4.8 collective-permute-start.43
  321.8 4.7 collective-permute-start.44
  331.5 10.7 %while.71 = (s32[]{:T(128)}, f32[16]{0:T(128)S(1)}, f32[24,128]{1,0:T(8,128)S(1)}, f32[24,128]{1,0:T(8,128)S(1)}, f32[3,24,128]{2,1,0:T(8,128)S(1)}, /*index=5*/...) while((s32[]{:T(128)}, f32[16]{0:T(128)S(1)}, ...), condition=%wide.region_25.26_spmd.clone, body=%wide.region_22.25_spmd.clone.sunk | while | flops 14286903 | bytes 3244889 | solution.py:73
  342.2 62.2 %psum.41 = f32[16]{0:T(128)S(1)} all-reduce(f32[16]{0:T(128)S(1)} %multiply_add_fusion.1), channel_id=1, replica_groups=mesh['sky'=16,'depth'=8] {'sky','depth'}, use_global_device_ids=true, to_apply=%region_26.27 | all-reduce | flops 16 | bytes 128 | tf_op jit(solution)/shard_map/psum | solution.py:203
  405.7 5.4 %fusion.43 = f32[16,128,128]{2,1,0:T(8,128)S(1)} fusion(f32[16]{0:T(128)S(1)} %get-tuple-element.1087, f32[16,128,128]{2,1,0:T(8,128)S(1)} %add_sqrt_fusion.4, f32[16]{0:T(128)S(1)} %add_multiply_fusion.4), kind=kLoop, calls=%fused_computation.111 | loop fusion | flops 29097984 | bytes 2097280 | tf_op jit(solution)/shard_map/reduce_sum | solution.py:46
  411.5 14.3 %while.69 = (s32[]{:T(128)}, f32[3,24,128]{2,1,0:T(8,128)S(1)}, f32[3,24,128]{2,1,0:T(8,128)S(1)}, f32[24,128]{1,0:T(8,128)S(1)}, f32[24,128]{1,0:T(8,128)S(1)},...) while((s32[]{:T(128)}, f32[3,24,128]{2,1,0:T(8,128)S(1)}, ...), condition=%wide.region_35.36_spmd.clone, body=%wide.region_30.0_spmd.clone.sunk | while | flops 18740276 | bytes 4916107 | solution.py:91
  430.7 3.3 collective-permute-start.53
  435.9 3.6 collective-permute-start.49
  440.3 3.8 collective-permute-start.55
  446.6 3.7 collective-permute-start.57
  450.2 5.3 %collective-permute-start.56 = (f32[3,3,128]{2,1,0:T(4,128)S(1)}, f32[3,3,128]{2,1,0:T(4,128)S(1)}, u32[]{:S(2)}, u32[]{:S(2)}) collective-permute-start(f32[3,3,128]{2,1,0:T(4,128)S(1)} %collective-permute-done.55), channel_id=1, source_target_pairs={{0,1},{1,2},{2,3},{3,4},{4,5},{5,6},{6,7},{8,9},{9,10},{10,11},{11... | collective-permute-start | bytes 13832 | tf_op jit(solution)/shard_map/ppermute | solution.py:23
  461.3 62.2 %psum.42 = f32[]{:T(128)} all-reduce(f32[]{:T(128)} %get-tuple-element.1161), channel_id=1, replica_groups=mesh['sky'=16,'depth'=8] {'sky','depth'}, use_global_device_ids=true, to_apply=%region_37.38 | all-reduce | flops 1 | bytes 8 | tf_op jit(solution)/shard_map/psum | solution.py:222
  (369 shorter events, 156.1 us)
Async XLA Ops:
  14.3 23.4 %collective-permute-start = (s32[3]{0:T(128)S(1)}, s32[3]{0:T(128)S(1)}, u32[]{:S(2)}, u32[]{:S(2)}) collective-permute-start(s32[3]{0:T(128)S(1)} %get-tuple-element.1142), channel_id=1, source_target_pairs={{0,8},{8,16},{16,24},{24,32},{32,40},{40,48},{48,56},{56,64},{64,7... | collective-permute-start | bytes 44 | tf_op jit(solution)/shard_map/ppermute | solution.py:17
  16.7 22.9 %collective-permute-start.2 = (s32[3]{0:T(128)S(1)}, s32[3]{0:T(128)S(1)}, u32[]{:S(2)}, u32[]{:S(2)}) collective-permute-start(s32[3]{0:T(128)S(1)} %get-tuple-element.1141), channel_id=1, source_target_pairs={{0,8},{8,16},{16,24},{24,32},{32,40},{40,48},{48,56},{56,64},{64,7... | collective-permute-start | bytes 44 | tf_op jit(solution)/shard_map/ppermute | solution.py:17
  18.4 26.1 %collective-permute-start.3 = (s32[3]{0:T(128)S(1)}, s32[3]{0:T(128)S(1)}, u32[]{:S(2)}, u32[]{:S(2)}) collective-permute-start(s32[3]{0:T(128)S(1)} %get-tuple-element.1140), channel_id=1, source_target_pairs={{0,8},{8,16},{16,24},{24,32},{32,40},{40,48},{48,56},{56,64},{64,7... | collective-permute-start | bytes 44 | tf_op jit(solution)/shard_map/ppermute | solution.py:17
  19.7 24.9 %collective-permute-start.5 = (s32[3]{0:T(128)S(1)}, s32[3]{0:T(128)S(1)}, u32[]{:S(2)}, u32[]{:S(2)}) collective-permute-start(s32[3]{0:T(128)S(1)} %get-tuple-element.1139), channel_id=1, source_target_pairs={{0,1},{1,2},{2,3},{3,4},{4,5},{5,6},{6,7},{8,9},{9,10},{10,11},{11... | collective-permute-start | bytes 44 | tf_op jit(solution)/shard_map/ppermute | solution.py:23
  26.4 44.1 %collective-permute-start.12 = (f32[3,3,128]{2,1,0:T(4,128)S(1)}, f32[3,3,128]{2,1,0:T(4,128)S(1)}, u32[]{:S(2)}, u32[]{:S(2)}) collective-permute-start(f32[3,3,128]{2,1,0:T(4,128)S(1)} %get-tuple-element.1133), channel_id=1, source_target_pairs={{0,8},{8,16},{16,24},{24,32},{32,40},{40,48},{48,56},{56,64},{64,7... | collective-permute-start | bytes 13832 | tf_op jit(solution)/shard_map/ppermute | solution.py:17
  44.7 33.7 %collective-permute-start.14 = (f32[3,3,128]{2,1,0:T(4,128)S(1)}, f32[3,3,128]{2,1,0:T(4,128)S(1)}, u32[]{:S(2)}, u32[]{:S(2)}) collective-permute-start(f32[3,3,128]{2,1,0:T(4,128)S(1)} %get-tuple-element.1132), channel_id=1, source_target_pairs={{0,8},{8,16},{16,24},{24,32},{32,40},{40,48},{48,56},{56,64},{64,7... | collective-permute-start | bytes 13832 | tf_op jit(solution)/shard_map/ppermute | solution.py:17
  46.1 33.1 %collective-permute-start.15 = (f32[3,3,128]{2,1,0:T(4,128)S(1)}, f32[3,3,128]{2,1,0:T(4,128)S(1)}, u32[]{:S(2)}, u32[]{:S(2)}) collective-permute-start(f32[3,3,128]{2,1,0:T(4,128)S(1)} %get-tuple-element.1131), channel_id=1, source_target_pairs={{0,8},{8,16},{16,24},{24,32},{32,40},{40,48},{48,56},{56,64},{64,7... | collective-permute-start | bytes 13832 | tf_op jit(solution)/shard_map/ppermute | solution.py:17
  47.4 44.3 %collective-permute-start.17 = (f32[3,3,128]{2,1,0:T(4,128)S(1)}, f32[3,3,128]{2,1,0:T(4,128)S(1)}, u32[]{:S(2)}, u32[]{:S(2)}) collective-permute-start(f32[3,3,128]{2,1,0:T(4,128)S(1)} %get-tuple-element.1130), channel_id=1, source_target_pairs={{0,1},{1,2},{2,3},{3,4},{4,5},{5,6},{6,7},{8,9},{9,10},{10,11},{11... | collective-permute-start | bytes 13832 | tf_op jit(solution)/shard_map/ppermute | solution.py:23
  68.5 23.3 %collective-permute-start.18 = (f32[3,3,128]{2,1,0:T(4,128)S(1)}, f32[3,3,128]{2,1,0:T(4,128)S(1)}, u32[]{:S(2)}, u32[]{:S(2)}) collective-permute-start(f32[3,3,128]{2,1,0:T(4,128)S(1)} %get-tuple-element.1129), channel_id=1, source_target_pairs={{1,0},{2,1},{3,2},{4,3},{5,4},{6,5},{7,6},{9,8},{10,9},{11,10},{12... | collective-permute-start | bytes 13832 | tf_op jit(solution)/shard_map/ppermute | solution.py:23
  79.2 10.6 %collective-permute-start.16 = (f32[3,3,128]{2,1,0:T(4,128)S(1)}, f32[3,3,128]{2,1,0:T(4,128)S(1)}, u32[]{:S(2)}, u32[]{:S(2)}) collective-permute-start(f32[3,3,128]{2,1,0:T(4,128)S(1)} %collective-permute-done.15), channel_id=1, source_target_pairs={{1,0},{2,1},{3,2},{4,3},{5,4},{6,5},{7,6},{9,8},{10,9},{11,10},{12... | collective-permute-start | bytes 13832 | tf_op jit(solution)/shard_map/ppermute | solution.py:23
  81.1 10.7 %collective-permute-start.21 = (f32[3,3,128]{2,1,0:T(4,128)S(1)}, f32[3,3,128]{2,1,0:T(4,128)S(1)}, u32[]{:S(2)}, u32[]{:S(2)}) collective-permute-start(f32[3,3,128]{2,1,0:T(4,128)S(1)} %get-tuple-element.1134), channel_id=1, source_target_pairs={{0,120},{8,0},{16,8},{24,16},{32,24},{40,32},{48,40},{56,48},{64,5... | collective-permute-start | bytes 13832 | tf_op jit(solution)/shard_map/ppermute | solution.py:17
  189.7 9.6 %collective-permute-start.24 = (f32[3,3,128]{2,1,0:T(4,128)S(1)}, f32[3,3,128]{2,1,0:T(4,128)S(1)}, u32[]{:S(2)}, u32[]{:S(2)}) collective-permute-start(f32[3,3,128]{2,1,0:T(4,128)S(1)} %get-tuple-element.1125), channel_id=1, source_target_pairs={{0,8},{8,16},{16,24},{24,32},{32,40},{40,48},{48,56},{56,64},{64,7... | collective-permute-start | bytes 13832 | tf_op jit(solution)/shard_map/ppermute | solution.py:17
  192.2 15.6 %collective-permute-start.26 = (f32[3,3,128]{2,1,0:T(4,128)S(1)}, f32[3,3,128]{2,1,0:T(4,128)S(1)}, u32[]{:S(2)}, u32[]{:S(2)}) collective-permute-start(f32[3,3,128]{2,1,0:T(4,128)S(1)} %get-tuple-element.1124), channel_id=1, source_target_pairs={{0,8},{8,16},{16,24},{24,32},{32,40},{40,48},{48,56},{56,64},{64,7... | collective-permute-start | bytes 13832 | tf_op jit(solution)/shard_map/ppermute | solution.py:17
  192.6 15.6 %collective-permute-start.27 = (f32[3,3,128]{2,1,0:T(4,128)S(1)}, f32[3,3,128]{2,1,0:T(4,128)S(1)}, u32[]{:S(2)}, u32[]{:S(2)}) collective-permute-start(f32[3,3,128]{2,1,0:T(4,128)S(1)} %get-tuple-element.1123), channel_id=1, source_target_pairs={{0,8},{8,16},{16,24},{24,32},{32,40},{40,48},{48,56},{56,64},{64,7... | collective-permute-start | bytes 13832 | tf_op jit(solution)/shard_map/ppermute | solution.py:17
  194.3 26.9 %collective-permute-start.29 = (f32[3,3,128]{2,1,0:T(4,128)S(1)}, f32[3,3,128]{2,1,0:T(4,128)S(1)}, u32[]{:S(2)}, u32[]{:S(2)}) collective-permute-start(f32[3,3,128]{2,1,0:T(4,128)S(1)} %get-tuple-element.1122), channel_id=1, source_target_pairs={{0,1},{1,2},{2,3},{3,4},{4,5},{5,6},{6,7},{8,9},{9,10},{10,11},{11... | collective-permute-start | bytes 13832 | tf_op jit(solution)/shard_map/ppermute | solution.py:23
  197.4 23.8 %collective-permute-start.30 = (f32[3,3,128]{2,1,0:T(4,128)S(1)}, f32[3,3,128]{2,1,0:T(4,128)S(1)}, u32[]{:S(2)}, u32[]{:S(2)}) collective-permute-start(f32[3,3,128]{2,1,0:T(4,128)S(1)} %get-tuple-element.1121), channel_id=1, source_target_pairs={{1,0},{2,1},{3,2},{4,3},{5,4},{6,5},{7,6},{9,8},{10,9},{11,10},{12... | collective-permute-start | bytes 13832 | tf_op jit(solution)/shard_map/ppermute | solution.py:23
  208.2 11.0 %collective-permute-start.28 = (f32[3,3,128]{2,1,0:T(4,128)S(1)}, f32[3,3,128]{2,1,0:T(4,128)S(1)}, u32[]{:S(2)}, u32[]{:S(2)}) collective-permute-start(f32[3,3,128]{2,1,0:T(4,128)S(1)} %collective-permute-done.27), channel_id=1, source_target_pairs={{1,0},{2,1},{3,2},{4,3},{5,4},{6,5},{7,6},{9,8},{10,9},{11,10},{12... | collective-permute-start | bytes 13832 | tf_op jit(solution)/shard_map/ppermute | solution.py:23
  210.2 11.1 %collective-permute-start.33 = (f32[3,3,128]{2,1,0:T(4,128)S(1)}, f32[3,3,128]{2,1,0:T(4,128)S(1)}, u32[]{:S(2)}, u32[]{:S(2)}) collective-permute-start(f32[3,3,128]{2,1,0:T(4,128)S(1)} %get-tuple-element.1126), channel_id=1, source_target_pairs={{0,120},{8,0},{16,8},{24,16},{32,24},{40,32},{48,40},{56,48},{64,5... | collective-permute-start | bytes 13832 | tf_op jit(solution)/shard_map/ppermute | solution.py:17
  296.3 14.7 %collective-permute-start.37 = (f32[3,3,128]{2,1,0:T(4,128)S(1)}, f32[3,3,128]{2,1,0:T(4,128)S(1)}, u32[]{:S(2)}, u32[]{:S(2)}) collective-permute-start(f32[3,3,128]{2,1,0:T(4,128)S(1)} %collective-permute-done.36), channel_id=1, source_target_pairs={{0,1},{1,2},{2,3},{3,4},{4,5},{5,6},{6,7},{8,9},{9,10},{10,11},{11... | collective-permute-start | bytes 13832 | tf_op jit(solution)/shard_map/ppermute | solution.py:23
  306.5 9.4 %collective-permute-start.38 = (f32[3,3,128]{2,1,0:T(4,128)S(1)}, f32[3,3,128]{2,1,0:T(4,128)S(1)}, u32[]{:S(2)}, u32[]{:S(2)}) collective-permute-start(f32[3,3,128]{2,1,0:T(4,128)S(1)} %bitcast.332), channel_id=1, source_target_pairs={{0,8},{8,16},{16,24},{24,32},{32,40},{40,48},{48,56},{56,64},{64,7... | collective-permute-start | bytes 13832 | tf_op jit(solution)/shard_map/ppermute | solution.py:17
  306.6 10.8 %collective-permute-start.39 = (f32[3,3,128]{2,1,0:T(4,128)S(1)}, f32[3,3,128]{2,1,0:T(4,128)S(1)}, u32[]{:S(2)}, u32[]{:S(2)}) collective-permute-start(f32[3,3,128]{2,1,0:T(4,128)S(1)} %bitcast.331), channel_id=1, source_target_pairs={{0,8},{8,16},{16,24},{24,32},{32,40},{40,48},{48,56},{56,64},{64,7... | collective-permute-start | bytes 13832 | tf_op jit(solution)/shard_map/ppermute | solution.py:17
  306.6 21.8 %collective-permute-start.41 = (f32[3,3,128]{2,1,0:T(4,128)S(1)}, f32[3,3,128]{2,1,0:T(4,128)S(1)}, u32[]{:S(2)}, u32[]{:S(2)}) collective-permute-start(f32[3,3,128]{2,1,0:T(4,128)S(1)} %bitcast.330), channel_id=1, source_target_pairs={{0,1},{1,2},{2,3},{3,4},{4,5},{5,6},{6,7},{8,9},{9,10},{10,11},{11... | collective-permute-start | bytes 13832 | tf_op jit(solution)/shard_map/ppermute | solution.py:23
  308.6 19.9 %collective-permute-start.42 = (f32[3,3,128]{2,1,0:T(4,128)S(1)}, f32[3,3,128]{2,1,0:T(4,128)S(1)}, u32[]{:S(2)}, u32[]{:S(2)}) collective-permute-start(f32[3,3,128]{2,1,0:T(4,128)S(1)} %bitcast.329), channel_id=1, source_target_pairs={{1,0},{2,1},{3,2},{4,3},{5,4},{6,5},{7,6},{9,8},{10,9},{11,10},{12... | collective-permute-start | bytes 13832 | tf_op jit(solution)/shard_map/ppermute | solution.py:23
  317.3 9.2 %collective-permute-start.40 = (f32[3,3,128]{2,1,0:T(4,128)S(1)}, f32[3,3,128]{2,1,0:T(4,128)S(1)}, u32[]{:S(2)}, u32[]{:S(2)}) collective-permute-start(f32[3,3,128]{2,1,0:T(4,128)S(1)} %collective-permute-done.39), channel_id=1, source_target_pairs={{1,0},{2,1},{3,2},{4,3},{5,4},{6,5},{7,6},{9,8},{10,9},{11,10},{12... | collective-permute-start | bytes 13832 | tf_op jit(solution)/shard_map/ppermute | solution.py:23
  319.3 9.3 %collective-permute-start.45 = (f32[3,3,128]{2,1,0:T(4,128)S(1)}, f32[3,3,128]{2,1,0:T(4,128)S(1)}, u32[]{:S(2)}, u32[]{:S(2)}) collective-permute-start(f32[3,3,128]{2,1,0:T(4,128)S(1)} %bitcast.328), channel_id=1, source_target_pairs={{0,120},{8,0},{16,8},{24,16},{32,24},{40,32},{48,40},{56,48},{64,5... | collective-permute-start | bytes 13832 | tf_op jit(solution)/shard_map/ppermute | solution.py:17
  425.8 10.1 %collective-permute-start.48 = (f32[3,3,128]{2,1,0:T(4,128)S(1)}, f32[3,3,128]{2,1,0:T(4,128)S(1)}, u32[]{:S(2)}, u32[]{:S(2)}) collective-permute-start(f32[3,3,128]{2,1,0:T(4,128)S(1)} %get-tuple-element.1109), channel_id=1, source_target_pairs={{0,8},{8,16},{16,24},{24,32},{32,40},{40,48},{48,56},{56,64},{64,7... | collective-permute-start | bytes 13832 | tf_op jit(solution)/shard_map/ppermute | solution.py:17
  428.5 15.6 %collective-permute-start.50 = (f32[3,3,128]{2,1,0:T(4,128)S(1)}, f32[3,3,128]{2,1,0:T(4,128)S(1)}, u32[]{:S(2)}, u32[]{:S(2)}) collective-permute-start(f32[3,3,128]{2,1,0:T(4,128)S(1)} %get-tuple-element.1108), channel_id=1, source_target_pairs={{0,8},{8,16},{16,24},{24,32},{32,40},{40,48},{48,56},{56,64},{64,7... | collective-permute-start | bytes 13832 | tf_op jit(solution)/shard_map/ppermute | solution.py:17
  428.7 15.9 %collective-permute-start.51 = (f32[3,3,128]{2,1,0:T(4,128)S(1)}, f32[3,3,128]{2,1,0:T(4,128)S(1)}, u32[]{:S(2)}, u32[]{:S(2)}) collective-permute-start(f32[3,3,128]{2,1,0:T(4,128)S(1)} %get-tuple-element.1107), channel_id=1, source_target_pairs={{0,8},{8,16},{16,24},{24,32},{32,40},{40,48},{48,56},{56,64},{64,7... | collective-permute-start | bytes 13832 | tf_op jit(solution)/shard_map/ppermute | solution.py:17
  430.7 26.9 %collective-permute-start.53 = (f32[3,3,128]{2,1,0:T(4,128)S(1)}, f32[3,3,128]{2,1,0:T(4,128)S(1)}, u32[]{:S(2)}, u32[]{:S(2)}) collective-permute-start(f32[3,3,128]{2,1,0:T(4,128)S(1)} %get-tuple-element.1106), channel_id=1, source_target_pairs={{0,1},{1,2},{2,3},{3,4},{4,5},{5,6},{6,7},{8,9},{9,10},{10,11},{11... | collective-permute-start | bytes 13832 | tf_op jit(solution)/shard_map/ppermute | solution.py:23
  434.0 23.5 %collective-permute-start.54 = (f32[3,3,128]{2,1,0:T(4,128)S(1)}, f32[3,3,128]{2,1,0:T(4,128)S(1)}, u32[]{:S(2)}, u32[]{:S(2)}) collective-permute-start(f32[3,3,128]{2,1,0:T(4,128)S(1)} %get-tuple-element.1105), channel_id=1, source_target_pairs={{1,0},{2,1},{3,2},{4,3},{5,4},{6,5},{7,6},{9,8},{10,9},{11,10},{12... | collective-permute-start | bytes 13832 | tf_op jit(solution)/shard_map/ppermute | solution.py:23
  444.6 10.9 %collective-permute-start.52 = (f32[3,3,128]{2,1,0:T(4,128)S(1)}, f32[3,3,128]{2,1,0:T(4,128)S(1)}, u32[]{:S(2)}, u32[]{:S(2)}) collective-permute-start(f32[3,3,128]{2,1,0:T(4,128)S(1)} %collective-permute-done.51), channel_id=1, source_target_pairs={{1,0},{2,1},{3,2},{4,3},{5,4},{6,5},{7,6},{9,8},{10,9},{11,10},{12... | collective-permute-start | bytes 13832 | tf_op jit(solution)/shard_map/ppermute | solution.py:23
  446.6 11.0 %collective-permute-start.57 = (f32[3,3,128]{2,1,0:T(4,128)S(1)}, f32[3,3,128]{2,1,0:T(4,128)S(1)}, u32[]{:S(2)}, u32[]{:S(2)}) collective-permute-start(f32[3,3,128]{2,1,0:T(4,128)S(1)} %get-tuple-element.1110), channel_id=1, source_target_pairs={{0,120},{8,0},{16,8},{24,16},{32,24},{40,32},{48,40},{56,48},{64,5... | collective-permute-start | bytes 13832 | tf_op jit(solution)/shard_map/ppermute | solution.py:17
  (34 other events, 369.4 us)
where the time goes:
time: 535 us; the launch traced here: 525 us
  blocking collectives  250 us (47%)
  starting transfers between devices  140 us (26%)
  other arithmetic  89.7 us (17%)
  waiting for transfers between devices  26.4 us (5%)
  local copies, waits for them, and re-layouts  12.1 us (2%)
    psum x2, blocking collectives, body(): counts = lax.psum(0.5 * self_total + ghost_total, ('sky', 'depth'))  125 us
    psum x2, blocking collectives, body(): lax.psum((jnp.sum(gradient * gradient), valid_local), ('sky', 'depth'))  124 us
    ppermute x30, starting transfers between devices, from_behind_2(): lax.ppermute(value, axis, [(source, source + steps) for source in range(i...  87.8 us
    ppermute x30, starting transfers between devices, from_behind(): lax.ppermute(array, axis, [(i, (i + by) % size) for i in range(size)])  52.4 us
    reduce_sum x8, other arithmetic, block_forces(): jnp.sum(bin_pull[:, None, None, None] * scaled * kernel, axis=0)  26.9 us
    reduce_sum x8, other arithmetic, block_counts(): return jnp.sum(weight[None] * kernel, axis=(1, 2, 3))  25.4 us
    ppermute x30, waiting for transfers between devices, from_behind_2(): lax.ppermute(value, axis, [(source, source + steps) for source in range(i...  21.5 us
  transfers between devices with their start and end apart: 60, of which 12 were waited for; matrix products, arithmetic and copies ran while one was open for 4% of the time, Pallas kernels for 0%

commit v1 on v0

v1 whole, which is shorter than its diff:
```python
import functools
import math

import jax
import jax.numpy as jnp
from jax import lax
from jax.experimental import pallas as pl
from jax.experimental.pallas import tpu as pltpu
from jax.sharding import PartitionSpec as P

STEPS = 2
EPS_SQ = 0.0001
STEP_SIZE = 0.01

BINS = 16
CELLS = 16
POINTS = 128
SLOTS = 3
AXES = ("sky", "depth")

UNIT = math.sqrt(128.0 * math.log2(math.e))
CENTRES = [(b + 0.5) / 16.0 for b in range(BINS)]
CHAIN = 4
LIFT = 64.0
MIDDLE = CENTRES[8]
RADIUS_CAP = 2.1 * UNIT
FAR = 1.0e4
COUNT_SCALE = [
    math.exp(16.0 * (b % CHAIN) * (MIDDLE - CENTRES[b - b % CHAIN]) - 0.5 * (b % CHAIN) ** 2) * 2.0**-LIFT
    for b in range(BINS)
]
FORCE_SCALE = [-256.0 / UNIT * scale for scale in COUNT_SCALE]

NEIGHBOURS = [(0, -1), (0, 1), (-1, 0), (-1, -1), (-1, 1), (1, 0), (1, -1), (1, 1)]
N_JOBS = 8 * SLOTS
STEP_ROWS = 16

VMEM = pl.BlockSpec(memory_space=pltpu.VMEM)
SMEM = pl.BlockSpec(memory_space=pltpu.SMEM)
PARAMS = pltpu.CompilerParams(vmem_limit_bytes=40 * 1024 * 1024)


def neighbour(across, along):
    sky_count, depth_count = lax.axis_size("sky"), lax.axis_size("depth")
    sky = lax.rem(lax.axis_index("sky") + (across + sky_count), sky_count)
    depth = lax.axis_index("depth") + along
    inside = (depth >= 0) & (depth < depth_count)
    return sky * depth_count + jnp.clip(depth, 0, depth_count - 1), inside


def column(values, shape):
    rows = lax.broadcasted_iota(jnp.int32, shape, 0)
    out = jnp.full(shape, values[0], jnp.float32)
    for index in range(1, len(values)):
        out = jnp.where(rows == index, values[index], out)
    return out


def pack(source, points, export_count, export_cell, import_pair, import_shift, outs):
    depth_up, depth_down, sky_up, sky_down = outs
    lanes = lax.broadcasted_iota(jnp.int32, (4, POINTS), 1)
    rows = lax.broadcasted_iota(jnp.int32, (4, POINTS), 0)
    for across in (-1, 0, 1):
        for along in (-1, 0, 1):
            if (across, along) == (0, 0):
                continue
            if along == 1:
                out = depth_up.at[across + 1]
            elif along == -1:
                out = depth_down.at[across + 1]
            else:
                out = sky_up if across == 1 else sky_down
            device, inside = neighbour(across, along)
            live = jnp.where(inside, export_count[0, device], 0)
            meta = jnp.zeros((4, POINTS), jnp.float32)
            for slot in range(SLOTS):
                right = export_cell[slot, device]
                out[slot] = source[right]
                size = jnp.where(slot < live, points[right], 0)
                meta = jnp.where(lanes == slot, size.astype(jnp.float32), meta)
                left = import_pair[slot, device]
                shift = jnp.zeros((4, POINTS), jnp.float32)
                for axis in range(3):
                    amount = import_shift[axis * SLOTS + slot, device].astype(jnp.float32) * UNIT
                    shift = jnp.where(rows == axis, amount, shift)
                out[SLOTS + slot] = source[left] - shift
                meta = jnp.where(lanes == SLOTS + slot, points[left].astype(jnp.float32), meta)
            out[2 * SLOTS] = meta


def first_kernel(
    positions, points, export_count, export_cell, import_pair, import_shift,
    target, depth_up, depth_down, sky_up, sky_down, source,
):
    lanes = lax.broadcasted_iota(jnp.int32, (4, POINTS), 1)
    for cell in range(CELLS):
        rows = [positions[axis, cell : cell + 1, :] for axis in range(3)]
        tile = jnp.concatenate(rows + [jnp.zeros((1, POINTS), jnp.float32)], axis=0) * UNIT
        live = lanes < points[cell]
        target[cell] = jnp.where(live, tile, -FAR)
        source[cell] = jnp.where(live, tile, FAR)
    pack(
        source, points, export_count, export_cell, import_pair, import_shift,
        (depth_up, depth_down, sky_up, sky_down),
    )


def add_pairs(job, slot, cell, size, target, source, force, counts):
    target_x = jnp.broadcast_to(target[cell, 0:1, :], (STEP_ROWS, POINTS))
    target_y = jnp.broadcast_to(target[cell, 1:2, :], (STEP_ROWS, POINTS))
    target_z = jnp.broadcast_to(target[cell, 2:3, :], (STEP_ROWS, POINTS))

    def step(index, unused):
        block = source[slot, pl.ds(pl.multiple_of(index * STEP_ROWS, STEP_ROWS), STEP_ROWS), :]
        dx = target_x - block[:, 0:1]
        dy = target_y - block[:, 1:2]
        dz = target_z - block[:, 2:3]
        square = dx * dx + dy * dy + dz * dz + EPS_SQ * UNIT * UNIT
        inverse = lax.rsqrt(square)
        radius = jnp.minimum(square * inverse, RADIUS_CAP)
        units = (dx * inverse, dy * inverse, dz * inverse)
        ratio = jnp.exp2(
            radius * (16.0 * math.log2(math.e) / UNIT) - 16.0 * math.log2(math.e) * MIDDLE
        )
        for chain in range(BINS // CHAIN):
            for link in range(CHAIN):
                b = chain * CHAIN + link
                delta = radius - CENTRES[b] * UNIT
                if link == 0:
                    value = jnp.exp2(LIFT - delta * delta)
                else:
                    value = value * ratio
                if counts is not None:
                    counts[b] += value[:8] + value[8:]
                slope = value * delta
                for axis in range(3):
                    pulled = slope * units[axis]
                    force[cell, axis * BINS + b] += pulled[:8] + pulled[8:]
        return unused

    lax.fori_loop(0, (size + (STEP_ROWS - 1)) // STEP_ROWS, step, 0)


def pair_kernel(
    target, points, export_count, export_cell, import_pair, import_shift,
    from_below, from_above, from_left, from_right,
    grad, payload, source, force, self_counts, pair_counts, meta, sems,
):
    lanes = lax.broadcasted_iota(jnp.int32, (4, POINTS), 1)
    rows = lax.broadcasted_iota(jnp.int32, (4, POINTS), 0)
    messages = [
        from_below.at[1], from_above.at[1],
        from_left.at[0], from_left.at[1], from_left.at[2],
        from_right.at[0], from_right.at[1], from_right.at[2],
    ]
    copies = [
        pltpu.make_async_copy(message.at[2 * SLOTS], meta.at[index], sems.at[index])
        for index, message in enumerate(messages)
    ]
    for copy in copies:
        copy.start()
    force[...] = jnp.zeros(force.shape, jnp.float32)
    self_counts[...] = jnp.zeros(self_counts.shape, jnp.float32)
    pair_counts[...] = jnp.zeros(pair_counts.shape, jnp.float32)

    def put(slot, tile):
        source[slot] = jnp.transpose(jnp.concatenate([tile, tile], axis=0), (1, 0))

    for cell in range(CELLS):
        put(cell, jnp.where(lanes < points[cell], target[cell], FAR))
    for index, (across, along) in enumerate(NEIGHBOURS):
        device, inside = neighbour(across, along)
        for slot in range(SLOTS):
            shift = jnp.zeros((4, POINTS), jnp.float32)
            for axis in range(3):
                amount = import_shift[axis * SLOTS + slot, device].astype(jnp.float32) * UNIT
                shift = jnp.where(rows == axis, amount, shift)
            put(CELLS + index * SLOTS + slot, messages[index][slot] + shift)
            put(CELLS + N_JOBS + index * SLOTS + slot, messages[index][SLOTS + slot])
    for copy in copies:
        copy.wait()

    def self_job(job, unused):
        add_pairs(job, job, job, points[job], target, source, force, self_counts)
        return unused

    lax.fori_loop(0, CELLS, self_job, 0)

    for index, (across, along) in enumerate(NEIGHBOURS):
        device, inside = neighbour(across, along)
        live = jnp.where(inside, export_count[0, device], 0)

        def import_job(slot, unused, index=index, device=device):
            size = meta[index, 0, slot].astype(jnp.int32)
            add_pairs(
                slot, CELLS + index * SLOTS + slot, import_pair[slot, device], size,
                target, source, force, pair_counts,
            )
            return unused

        def export_job(slot, unused, index=index, device=device, live=live):
            size = meta[index, 0, SLOTS + slot].astype(jnp.int32)
            add_pairs(
                slot, CELLS + N_JOBS + index * SLOTS + slot, export_cell[slot, device], size,
                target, source, force, None,
            )
            return unused

        lax.fori_loop(0, SLOTS, import_job, 0)
        lax.fori_loop(0, live, export_job, 0)

    force_scale = column(FORCE_SCALE, (BINS, POINTS))
    for cell in range(CELLS):
        for axis in range(3):
            tile = jnp.sum(force[cell, axis * BINS : (axis + 1) * BINS], axis=1) * force_scale
            at = (cell * 3 + axis) * POINTS
            grad[:, at : at + POINTS] = tile
    whole = grad[...]
    gram = lax.dot_general(
        whole, whole, (((1,), (1,)), ((), ())),
        precision=lax.Precision.HIGHEST, preferred_element_type=jnp.float32,
    )
    bins = lax.broadcasted_iota(jnp.int32, (BINS, POINTS), 0)
    lane = lax.broadcasted_iota(jnp.int32, (BINS, POINTS), 1)
    low, high = lane % BINS, lane // BINS
    spread = jnp.where(low == bins, 1.0, 0.0)
    wide = lax.dot_general(
        gram, spread, (((1,), (0,)), ((), ())),
        precision=lax.Precision.HIGHEST, preferred_element_type=jnp.float32,
    )
    first = jnp.sum(jnp.where(bins == (low + high) % BINS, wide, 0.0), axis=0, keepdims=True)
    second = jnp.where((bins == (low + 8) % BINS) & (high == 0), wide, 0.0)
    sums = jnp.sum(0.5 * self_counts[...] + pair_counts[...], axis=1)
    sums = jnp.sum(sums, axis=1, keepdims=True) * column(COUNT_SCALE, (BINS, POINTS))
    second = second + jnp.where(lane == bins + BINS, sums, 0.0)
    total = points[0]
    for cell in range(1, CELLS):
        total = total + points[cell]
    second = second + jnp.where((lane == 2 * BINS) & (bins == 0), total.astype(jnp.float32), 0.0)
    second = jnp.sum(second, axis=0, keepdims=True)
    both = jnp.concatenate([first, second], axis=0)
    payload[...] = jnp.broadcast_to(both[None], payload.shape)


def moves_of(sums, grad, target_log):
    both = jnp.sum(sums[...], axis=0)
    bins = lax.broadcasted_iota(jnp.int32, (BINS, POINTS), 0)
    lane = lax.broadcasted_iota(jnp.int32, (BINS, POINTS), 1)
    low, high = lane % BINS, lane // BINS
    first, second = both[0:1], both[1:2]
    counts = jnp.sum(
        jnp.where(lane == bins + BINS, jnp.broadcast_to(second, (BINS, POINTS)), 0.0), axis=1, keepdims=True
    )
    counts = jnp.broadcast_to(counts, (BINS, POINTS))
    one_lane = lax.broadcasted_iota(jnp.int32, (1, POINTS), 1)
    valid = jnp.sum(jnp.where(one_lane == 2 * BINS, second, 0.0), axis=1, keepdims=True)
    mean_count = jnp.sum(counts, axis=0, keepdims=True) / BINS
    logs = column([target_log[b] for b in range(BINS)], (BINS, POINTS))
    pull = (jnp.log(1.0 + counts) - logs) * mean_count / (1.0 + counts)
    here = jnp.sum(jnp.where(bins == low, pull, 0.0), axis=0, keepdims=True)
    there = jnp.sum(jnp.where(bins == (low + high) % BINS, pull, 0.0), axis=0, keepdims=True)
    across = jnp.sum(jnp.where(bins == (low + 8) % BINS, pull, 0.0), axis=0, keepdims=True)
    power = first * here * there * jnp.where(one_lane < BINS, 1.0, 2.0)
    power = power + jnp.where(one_lane < BINS, second * here * across, 0.0)
    power = jnp.maximum(jnp.sum(power, axis=1, keepdims=True), 0.0)
    rms = jnp.sqrt(power / (3.0 * valid) + 1e-06)
    weights = pull / -rms
    out = []
    for cell in range(CELLS):
        parts = []
        for axis in range(3):
            at = (cell * 3 + axis) * POINTS
            parts.append(jnp.sum(grad[:, at : at + POINTS] * weights, axis=0, keepdims=True))
        out.append(parts)
    return out


def update_kernel(
    sums, grad, target, target_log, points, export_count, export_cell, import_pair, import_shift,
    travel, next_target, depth_up, depth_down, sky_up, sky_down, source,
):
    lanes = lax.broadcasted_iota(jnp.int32, (4, POINTS), 1)
    moves = moves_of(sums, grad, target_log)
    for cell in range(CELLS):
        tile = jnp.concatenate(moves[cell] + [jnp.zeros((1, POINTS), jnp.float32)], axis=0)
        travel[cell] = tile
        tile = target[cell] + (STEP_SIZE * UNIT) * tile
        next_target[cell] = tile
        source[cell] = jnp.where(lanes < points[cell], tile, FAR)
    pack(
        source, points, export_count, export_cell, import_pair, import_shift,
        (depth_up, depth_down, sky_up, sky_down),
    )


def last_kernel(sums, grad, travel, target_log, out):
    moves = moves_of(sums, grad, target_log)
    for cell in range(CELLS):
        for axis in range(3):
            out[axis, cell : cell + 1, :] = travel[cell, axis : axis + 1, :] + moves[cell][axis]


def f32(*shape):
    return jax.ShapeDtypeStruct(shape, jnp.float32)


CELL_SHAPE = (CELLS, 4, POINTS)
GRAD_SHAPE = (BINS, CELLS * 3 * POINTS)
MESSAGE = (2 * SLOTS + 1, 4, POINTS)
MESSAGES = [f32(3, *MESSAGE), f32(3, *MESSAGE), f32(*MESSAGE), f32(*MESSAGE)]


def along_depth(value, by):
    count = lax.axis_size("depth")
    return lax.ppermute(value, "depth", [(i, i + by) for i in range(count) if 0 <= i + by < count])


def along_sky(value, by):
    count = lax.axis_size("sky")
    return lax.ppermute(value, "sky", [(i, (i + by) % count) for i in range(count)])


def body(positions, cell_points, target_log, export_count, export_cell, import_pair, import_shift):
    devices = export_count.shape[1]
    tables = (
        cell_points,
        export_count,
        jnp.transpose(export_cell[0], (1, 0)),
        jnp.transpose(import_pair[0], (1, 0)),
        jnp.transpose(import_shift[:, 0], (0, 2, 1)).reshape(3 * SLOTS, devices),
    )
    target, *messages = pl.pallas_call(
        first_kernel,
        out_shape=[f32(*CELL_SHAPE)] + MESSAGES,
        in_specs=[VMEM] + [SMEM] * 5,
        out_specs=[VMEM] * 5,
        scratch_shapes=[pltpu.VMEM(CELL_SHAPE, jnp.float32)],
        compiler_params=PARAMS,
        name="first",
    )(positions, *tables)
    for iteration in range(STEPS):
        depth_up, depth_down, sky_up, sky_down = messages
        from_below = along_depth(depth_up, 1)
        from_above = along_depth(depth_down, -1)
        from_left = along_sky(jnp.stack([sky_up, from_below[2], from_above[2]]), 1)
        from_right = along_sky(jnp.stack([sky_down, from_below[0], from_above[0]]), -1)
        grad, payload = pl.pallas_call(
            pair_kernel,
            out_shape=[f32(*GRAD_SHAPE), f32(devices, 2, POINTS)],
            in_specs=[VMEM] + [SMEM] * 5 + [VMEM] * 4,
            out_specs=[VMEM] * 2,
            scratch_shapes=[
                pltpu.VMEM((CELLS + 2 * N_JOBS, POINTS, 8), jnp.float32),
                pltpu.VMEM((CELLS, 3 * BINS, 8, POINTS), jnp.float32),
                pltpu.VMEM((BINS, 8, POINTS), jnp.float32),
                pltpu.VMEM((BINS, 8, POINTS), jnp.float32),
                pltpu.SMEM((8, 4, POINTS), jnp.float32),
                pltpu.SemaphoreType.DMA((8,)),
            ],
            compiler_params=PARAMS,
            name="pairs",
        )(target, *tables, from_below, from_above, from_left, from_right)
        sums = lax.all_to_all(payload, AXES, 0, 0)
        if iteration == STEPS - 1:
            return pl.pallas_call(
                last_kernel,
                out_shape=f32(*positions.shape),
                in_specs=[VMEM] * 3 + [SMEM],
                out_specs=VMEM,
                compiler_params=PARAMS,
                name="last",
            )(sums, grad, travel, target_log)
        travel, target, *messages = pl.pallas_call(
            update_kernel,
            out_shape=[f32(*CELL_SHAPE), f32(*CELL_SHAPE)] + MESSAGES,
            in_specs=[VMEM] * 3 + [SMEM] * 6,
            out_specs=[VMEM] * 6,
            scratch_shapes=[pltpu.VMEM(CELL_SHAPE, jnp.float32)],
            compiler_params=PARAMS,
            name="update",
        )(sums, grad, target, target_log, *tables)


def solution(mesh):
    in_specs = (
        P(None, ("sky", "depth"), None),
        P(("sky", "depth")),
        P(),
        P(("sky", "depth"), None),
        P(("sky", "depth"), None, None),
        P(("sky", "depth"), None, None),
        P(None, ("sky", "depth"), None, None),
    )
    out_specs = P(None, ("sky", "depth"), None)
    return jax.shard_map(body, mesh=mesh, in_specs=in_specs, out_specs=out_specs, check_vma=False)
```

time: 535 us -> 145 us (0.27); the launches traced: 525 us -> 146 us
  blocking collectives: 250 us -> 51.7 us
  starting transfers between devices: 140 us -> 22.3 us
  other arithmetic: 89.7 us -> 0.05 us
  Pallas kernels: 0 us -> 59.3 us
  waiting for transfers between devices: 26.4 us -> 9.43 us
  local copies, waits for them, and re-layouts: 12.1 us -> 3.4 us
    psum x4 -> x0, blocking collectives: 250 us -> none  [the longest x2 125 us: body(): counts = lax.psum(0.5 * self_total + ghost_total, ('sky', 'depth'))]
    ppermute x60 -> x8, starting transfers between devices: 140 us -> 22.3 us  [the longest x4 11.2 us: along_depth(): lax.ppermute(value, 'depth', [(i, i + by) for i in range(count) if 0 <= i...]
    reduce_sum x41 -> x0, other arithmetic: 72.1 us -> none  [the longest x8 26.9 us: block_forces(): jnp.sum(bin_pull[:, None, None, None] * scaled * kernel, axis=0)]
    pallas_call x0 -> x5, Pallas kernels: none -> 59.3 us  [the longest x2 55.4 us: body(): pl.pallas_call(pair_kernel, out_shape=[f32(*GRAD_SHAPE), f32(devices, 2,...]
    all_to_all x0 -> x2, blocking collectives: none -> 51.7 us  [body(): sums = lax.all_to_all(payload, AXES, 0, 0)]
    ppermute x60 -> x8, waiting for transfers between devices: 26.4 us -> 9.43 us  [the longest x4 6.79 us: along_depth(): lax.ppermute(value, 'depth', [(i, i + by) for i in range(count) if 0 <= i...]
    select_n x4 -> x0, other arithmetic: 10.6 us -> none  [the longest x1 10.6 us: body(): sizes_out = jnp.where(live_out, cell_points[export_cell[0]], 0)]
    gather x11 -> x0, local copies, waits for them, and re-layouts: 8.48 us -> none  [the longest x2 1.95 us: send_cells(): coords[:, export_row[near_ids].reshape(-1)]]
  transfers between devices with their start and end apart: 60 -> 8, of which waited for: 12 -> 4; matrix products, arithmetic and copies ran while one was open for 4% -> 0% of each run, Pallas kernels for 0% -> 0%
where the time goes in v1:
time: 145 us; the launch traced here: 146 us
  Pallas kernels  59.3 us (41%)
  blocking collectives  51.7 us (36%)
  starting transfers between devices  22.3 us (15%)
  waiting for transfers between devices  9.43 us (7%)
  local copies, waits for them, and re-layouts  3.4 us (2%)
    pallas_call x2, Pallas kernels, body(): pl.pallas_call(pair_kernel, out_shape=[f32(*GRAD_SHAPE), f32(devices, 2,...  55.4 us
    all_to_all x2, blocking collectives, body(): sums = lax.all_to_all(payload, AXES, 0, 0)  51.7 us
    ppermute x4, starting transfers between devices, along_depth(): lax.ppermute(value, 'depth', [(i, i + by) for i in range(count) if 0 <= i...  11.2 us
    ppermute x4, starting transfers between devices, along_sky(): lax.ppermute(value, 'sky', [(i, (i + by) % count) for i in range(count)])  11 us
    ppermute x4, waiting for transfers between devices, along_depth(): lax.ppermute(value, 'depth', [(i, i + by) for i in range(count) if 0 <= i...  6.79 us
  transfers between devices with their start and end apart: 8, of which 4 were waited for; matrix products, arithmetic and copies ran while one was open for 0% of the time, Pallas kernels for 0%

profile of v1, /device:TPU:1, one launch (start us, length us, event | category | flops | bytes accessed | tf_op | source)
XLA Modules:
  0.0 146.3 jit_solution(5383253810480840900)
XLA Ops:
  0.0 0.0 copy-start
  0.0 0.7 copy.14
  0.7 0.0 copy-start.4
  0.7 0.7 copy-done.4
  1.4 0.7 copy_bitcast_fusion.1
  2.1 0.0 copy-done
  2.1 0.6 copy-done.1
  2.7 0.0 copy-done.2
  2.7 1.0 first.1
  3.7 4.6 %collective-permute-start = (f32[3,7,4,128]{3,2,1,0:T(4,128)S(1)}, f32[3,7,4,128]{3,2,1,0:T(4,128)S(1)}, u32[]{:S(2)}, u32[]{:S(2)}) collective-permute-start(f32[3,7,4,128]{3,2,1,0:T(4,128)S(1)} %get-tuple-element.21), channel_id=1, source_target_pairs={{0,1},{1,2},{2,3},{3,4},{4,5},{5,6},{6,7},{8,9},{9,10},{10,11},{11... | collective-permute-start | bytes 129032 | tf_op jit(solution)/shard_map/ppermute | solution.py:315
  8.3 1.9 %collective-permute-start.1 = (f32[3,7,4,128]{3,2,1,0:T(4,128)S(1)}, f32[3,7,4,128]{3,2,1,0:T(4,128)S(1)}, u32[]{:S(2)}, u32[]{:S(2)}) collective-permute-start(f32[3,7,4,128]{3,2,1,0:T(4,128)S(1)} %get-tuple-element.22), channel_id=1, source_target_pairs={{1,0},{2,1},{3,2},{4,3},{5,4},{6,5},{7,6},{9,8},{10,9},{11,10},{12... | collective-permute-start | bytes 129032 | tf_op jit(solution)/shard_map/ppermute | solution.py:315
  10.2 0.0 collective-permute-done.from_below
  10.3 3.4 %collective-permute-done.1.from_above = f32[3,7,4,128]{3,2,1,0:T(4,128)S(1)} collective-permute-done((f32[3,7,4,128]{3,2,1,0:T(4,128)S(1)}, f32[3,7,4,128]{3,2,1,0:T(4,128)S(1)}, u32[]{:S(2)}, u32[]{:S(2)}) %collective-permute-start.1) | collective-permute-done | bytes 43040 | tf_op jit(solution)/shard_map/ppermute | solution.py:315
  13.7 1.7 %collective-permute-start.2 = (f32[3,7,4,128]{3,2,1,0:T(4,128)S(1)}, f32[3,7,4,128]{3,2,1,0:T(4,128)S(1)}, u32[]{:S(2)}, u32[]{:S(2)}) collective-permute-start(f32[3,7,4,128]{3,2,1,0:T(4,128)S(1)} %pad_maximum_fusion), channel_id=1, source_target_pairs={{0,8},{8,16},{16,24},{24,32},{32,40},{40,48},{48,56},{56,64},{64,7... | collective-permute-start | bytes 129032 | tf_op jit(solution)/shard_map/ppermute | solution.py:320
  15.4 4.4 %collective-permute-start.3 = (f32[3,7,4,128]{3,2,1,0:T(4,128)S(1)}, f32[3,7,4,128]{3,2,1,0:T(4,128)S(1)}, u32[]{:S(2)}, u32[]{:S(2)}) collective-permute-start(f32[3,7,4,128]{3,2,1,0:T(4,128)S(1)} %pad_maximum_fusion.1), channel_id=1, source_target_pairs={{0,120},{8,0},{16,8},{24,16},{32,24},{40,32},{48,40},{56,48},{64,5... | collective-permute-start | bytes 129032 | tf_op jit(solution)/shard_map/ppermute | solution.py:320
  19.8 1.3 collective-permute-done.2.from_left
  21.1 0.0 collective-permute-done.3.from_right
  21.1 27.7 %pairs.2 = (f32[16,6144]{1,0:T(8,128)S(1)}, f32[128,2,128]{2,1,0:T(2,128)S(1)}) custom-call(f32[16,4,128]{2,1,0:T(4,128)S(1)} %get-tuple-element.20.target, s32[16]{0:T(128)S(1)} %copy-done.1, s32[1,128]{1,0:T(1,128)S(1)} %copy-done.2, s32[3,128]{1,0:T(4,128)S(1)} %get-tuple-element.44.export_cell, s32[3,128]{1,0:T(4,128)S(1)} %get-tuple-element.43.import_pair, ...), custom_call_target="tpu_custom_call" | custom-call | tf_op jit(solution)/shard_map/pairs/pallas_call | solution.py:347
  48.8 26.2 %all_to_all.10.sums = f32[128,2,128]{2,1,0:T(2,128)S(1)} all-to-all(f32[128,2,128]{2,1,0:T(2,128)S(1)} %get-tuple-element.25), channel_id=1, replica_groups=mesh['sky'=16,'depth'=8] {'sky','depth'}, dimensions={0} | all-to-all | bytes 262144 | tf_op jit(solution)/shard_map/all_to_all | solution.py:363
  75.1 0.7 copy-done.3
  75.7 1.4 update.1
  77.1 2.8 %collective-permute-start.4 = (f32[3,7,4,128]{3,2,1,0:T(4,128)S(1)}, f32[3,7,4,128]{3,2,1,0:T(4,128)S(1)}, u32[]{:S(2)}, u32[]{:S(2)}) collective-permute-start(f32[3,7,4,128]{3,2,1,0:T(4,128)S(1)} %get-tuple-element.28), channel_id=1, source_target_pairs={{0,1},{1,2},{2,3},{3,4},{4,5},{5,6},{6,7},{8,9},{9,10},{10,11},{11... | collective-permute-start | bytes 129032 | tf_op jit(solution)/shard_map/ppermute | solution.py:315
  79.9 1.9 %collective-permute-start.5 = (f32[3,7,4,128]{3,2,1,0:T(4,128)S(1)}, f32[3,7,4,128]{3,2,1,0:T(4,128)S(1)}, u32[]{:S(2)}, u32[]{:S(2)}) collective-permute-start(f32[3,7,4,128]{3,2,1,0:T(4,128)S(1)} %get-tuple-element.29), channel_id=1, source_target_pairs={{1,0},{2,1},{3,2},{4,3},{5,4},{6,5},{7,6},{9,8},{10,9},{11,10},{12... | collective-permute-start | bytes 129032 | tf_op jit(solution)/shard_map/ppermute | solution.py:315
  81.8 0.0 collective-permute-done.4.from_below
  81.8 3.4 %collective-permute-done.5.from_above = f32[3,7,4,128]{3,2,1,0:T(4,128)S(1)} collective-permute-done((f32[3,7,4,128]{3,2,1,0:T(4,128)S(1)}, f32[3,7,4,128]{3,2,1,0:T(4,128)S(1)}, u32[]{:S(2)}, u32[]{:S(2)}) %collective-permute-start.5) | collective-permute-done | bytes 43040 | tf_op jit(solution)/shard_map/ppermute | solution.py:315
  85.2 0.1 collective-permute-start.6
  85.4 4.8 %collective-permute-start.7 = (f32[3,7,4,128]{3,2,1,0:T(4,128)S(1)}, f32[3,7,4,128]{3,2,1,0:T(4,128)S(1)}, u32[]{:S(2)}, u32[]{:S(2)}) collective-permute-start(f32[3,7,4,128]{3,2,1,0:T(4,128)S(1)} %pad_maximum_fusion.3), channel_id=1, source_target_pairs={{0,120},{8,0},{16,8},{24,16},{32,24},{40,32},{48,40},{56,48},{64,5... | collective-permute-start | bytes 129032 | tf_op jit(solution)/shard_map/ppermute | solution.py:320
  90.2 1.3 collective-permute-done.6.from_left
  91.5 0.0 collective-permute-done.7.from_right
  91.5 27.7 %pairs.3 = (f32[16,6144]{1,0:T(8,128)S(1)}, f32[128,2,128]{2,1,0:T(2,128)S(1)}) custom-call(f32[16,4,128]{2,1,0:T(4,128)S(1)} %get-tuple-element.27.target, s32[16]{0:T(128)S(1)} %copy-done.1, s32[1,128]{1,0:T(1,128)S(1)} %copy-done.2, s32[3,128]{1,0:T(4,128)S(1)} %get-tuple-element.44.export_cell, s32[3,128]{1,0:T(4,128)S(1)} %get-tuple-element.43.import_pair, ...), custom_call_target="tpu_custom_call" | custom-call | tf_op jit(solution)/shard_map/pairs/pallas_call | solution.py:347
  119.2 25.5 %all_to_all.11.sums = f32[128,2,128]{2,1,0:T(2,128)S(1)} all-to-all(f32[128,2,128]{2,1,0:T(2,128)S(1)} %get-tuple-element.32), channel_id=1, replica_groups=mesh['sky'=16,'depth'=8] {'sky','depth'}, dimensions={0} | all-to-all | bytes 262144 | tf_op jit(solution)/shard_map/all_to_all | solution.py:363
  144.7 1.6 %last.1 = f32[3,16,128]{2,1,0:T(8,128)} custom-call(f32[128,2,128]{2,1,0:T(2,128)S(1)} %all_to_all.11.sums, f32[16,6144]{1,0:T(8,128)S(1)} %get-tuple-element.33.grad, f32[16,4,128]{2,1,0:T(4,128)S(1)} %get-tuple-element.34.travel, f32[16]{0:T(128)S(1)} %copy-done.3), custom_call_target="tpu_custom_call" | custom-call | tf_op jit(solution)/shard_map/last/pallas_call | solution.py:365
  (12 shorter events, 0.1 us)
Async XLA Ops:
  0.0 2.1 %copy-start = (f32[3,16,128]{2,1,0:T(8,128)S(1)}, f32[3,16,128]{2,1,0:T(8,128)}, u32[]{:S(2)}) copy-start(f32[3,16,128]{2,1,0:T(8,128)} %positions.1) | copy-start | bytes 73732
  0.7 0.7 copy-start.4
  2.1 0.7 copy-start.1
  2.1 0.7 copy-start.2
  3.7 6.5 %collective-permute-start = (f32[3,7,4,128]{3,2,1,0:T(4,128)S(1)}, f32[3,7,4,128]{3,2,1,0:T(4,128)S(1)}, u32[]{:S(2)}, u32[]{:S(2)}) collective-permute-start(f32[3,7,4,128]{3,2,1,0:T(4,128)S(1)} %get-tuple-element.21), channel_id=1, source_target_pairs={{0,1},{1,2},{2,3},{3,4},{4,5},{5,6},{6,7},{8,9},{9,10},{10,11},{11... | collective-permute-start | bytes 129032 | tf_op jit(solution)/shard_map/ppermute | solution.py:315
  8.3 5.3 %collective-permute-start.1 = (f32[3,7,4,128]{3,2,1,0:T(4,128)S(1)}, f32[3,7,4,128]{3,2,1,0:T(4,128)S(1)}, u32[]{:S(2)}, u32[]{:S(2)}) collective-permute-start(f32[3,7,4,128]{3,2,1,0:T(4,128)S(1)} %get-tuple-element.22), channel_id=1, source_target_pairs={{1,0},{2,1},{3,2},{4,3},{5,4},{6,5},{7,6},{9,8},{10,9},{11,10},{12... | collective-permute-start | bytes 129032 | tf_op jit(solution)/shard_map/ppermute | solution.py:315
  13.7 7.4 %collective-permute-start.2 = (f32[3,7,4,128]{3,2,1,0:T(4,128)S(1)}, f32[3,7,4,128]{3,2,1,0:T(4,128)S(1)}, u32[]{:S(2)}, u32[]{:S(2)}) collective-permute-start(f32[3,7,4,128]{3,2,1,0:T(4,128)S(1)} %pad_maximum_fusion), channel_id=1, source_target_pairs={{0,8},{8,16},{16,24},{24,32},{32,40},{40,48},{48,56},{56,64},{64,7... | collective-permute-start | bytes 129032 | tf_op jit(solution)/shard_map/ppermute | solution.py:320
  15.4 5.7 %collective-permute-start.3 = (f32[3,7,4,128]{3,2,1,0:T(4,128)S(1)}, f32[3,7,4,128]{3,2,1,0:T(4,128)S(1)}, u32[]{:S(2)}, u32[]{:S(2)}) collective-permute-start(f32[3,7,4,128]{3,2,1,0:T(4,128)S(1)} %pad_maximum_fusion.1), channel_id=1, source_target_pairs={{0,120},{8,0},{16,8},{24,16},{32,24},{40,32},{48,40},{56,48},{64,5... | collective-permute-start | bytes 129032 | tf_op jit(solution)/shard_map/ppermute | solution.py:320
  75.1 0.7 copy-start.3
  77.1 4.7 %collective-permute-start.4 = (f32[3,7,4,128]{3,2,1,0:T(4,128)S(1)}, f32[3,7,4,128]{3,2,1,0:T(4,128)S(1)}, u32[]{:S(2)}, u32[]{:S(2)}) collective-permute-start(f32[3,7,4,128]{3,2,1,0:T(4,128)S(1)} %get-tuple-element.28), channel_id=1, source_target_pairs={{0,1},{1,2},{2,3},{3,4},{4,5},{5,6},{6,7},{8,9},{9,10},{10,11},{11... | collective-permute-start | bytes 129032 | tf_op jit(solution)/shard_map/ppermute | solution.py:315
  79.9 5.3 %collective-permute-start.5 = (f32[3,7,4,128]{3,2,1,0:T(4,128)S(1)}, f32[3,7,4,128]{3,2,1,0:T(4,128)S(1)}, u32[]{:S(2)}, u32[]{:S(2)}) collective-permute-start(f32[3,7,4,128]{3,2,1,0:T(4,128)S(1)} %get-tuple-element.29), channel_id=1, source_target_pairs={{1,0},{2,1},{3,2},{4,3},{5,4},{6,5},{7,6},{9,8},{10,9},{11,10},{12... | collective-permute-start | bytes 129032 | tf_op jit(solution)/shard_map/ppermute | solution.py:315
  85.2 6.3 %collective-permute-start.6 = (f32[3,7,4,128]{3,2,1,0:T(4,128)S(1)}, f32[3,7,4,128]{3,2,1,0:T(4,128)S(1)}, u32[]{:S(2)}, u32[]{:S(2)}) collective-permute-start(f32[3,7,4,128]{3,2,1,0:T(4,128)S(1)} %pad_maximum_fusion.2), channel_id=1, source_target_pairs={{0,8},{8,16},{16,24},{24,32},{32,40},{40,48},{48,56},{56,64},{64,7... | collective-permute-start | bytes 129032 | tf_op jit(solution)/shard_map/ppermute | solution.py:320
  85.4 6.1 %collective-permute-start.7 = (f32[3,7,4,128]{3,2,1,0:T(4,128)S(1)}, f32[3,7,4,128]{3,2,1,0:T(4,128)S(1)}, u32[]{:S(2)}, u32[]{:S(2)}) collective-permute-start(f32[3,7,4,128]{3,2,1,0:T(4,128)S(1)} %pad_maximum_fusion.3), channel_id=1, source_target_pairs={{0,120},{8,0},{16,8},{24,16},{32,24},{40,32},{48,40},{56,48},{64,5... | collective-permute-start | bytes 129032 | tf_op jit(solution)/shard_map/ppermute | solution.py:320

commit v2 on v1

--- a/solution.py
+++ b/solution.py
@@ -32,8 +32,9 @@
 FORCE_SCALE = [-256.0 / UNIT * scale for scale in COUNT_SCALE]
 
 NEIGHBOURS = [(0, -1), (0, 1), (-1, 0), (-1, -1), (-1, 1), (1, 0), (1, -1), (1, 1)]
-N_JOBS = 8 * SLOTS
 STEP_ROWS = 16
+BLOCKS = POINTS // STEP_ROWS
+UNROLL = 2
 
 VMEM = pl.BlockSpec(memory_space=pltpu.VMEM)
 SMEM = pl.BlockSpec(memory_space=pltpu.SMEM)
@@ -105,110 +106,166 @@
     )
 
 
-def add_pairs(job, slot, cell, size, target, source, force, counts):
-    target_x = jnp.broadcast_to(target[cell, 0:1, :], (STEP_ROWS, POINTS))
-    target_y = jnp.broadcast_to(target[cell, 1:2, :], (STEP_ROWS, POINTS))
-    target_z = jnp.broadcast_to(target[cell, 2:3, :], (STEP_ROWS, POINTS))
-
-    def step(index, unused):
-        block = source[slot, pl.ds(pl.multiple_of(index * STEP_ROWS, STEP_ROWS), STEP_ROWS), :]
-        dx = target_x - block[:, 0:1]
-        dy = target_y - block[:, 1:2]
-        dz = target_z - block[:, 2:3]
+def spread_points(at, row_list, source, base, spread):
+    blocks = [
+        source[pl.ds(pl.multiple_of(row_list[at + unit] * STEP_ROWS, STEP_ROWS), STEP_ROWS), :]
+        for unit in range(UNROLL)
+    ]
+    for axis in range(3):
+        for unit in range(UNROLL):
+            lane = base + axis
+            spread[unit, axis] = jnp.broadcast_to(blocks[unit][:, lane : lane + 1], (STEP_ROWS, POINTS))
+
+
+def shape_pairs(at, cell_list, target, spread, shapes):
+    for unit in range(UNROLL):
+        cell = cell_list[at + unit]
+        dx, dy, dz = (target[cell, axis : axis + 1, :] - spread[unit, axis] for axis in range(3))
         square = dx * dx + dy * dy + dz * dz + EPS_SQ * UNIT * UNIT
         inverse = lax.rsqrt(square)
         radius = jnp.minimum(square * inverse, RADIUS_CAP)
-        units = (dx * inverse, dy * inverse, dz * inverse)
         ratio = jnp.exp2(
             radius * (16.0 * math.log2(math.e) / UNIT) - 16.0 * math.log2(math.e) * MIDDLE
         )
-        for chain in range(BINS // CHAIN):
-            for link in range(CHAIN):
-                b = chain * CHAIN + link
-                delta = radius - CENTRES[b] * UNIT
-                if link == 0:
-                    value = jnp.exp2(LIFT - delta * delta)
-                else:
-                    value = value * ratio
-                if counts is not None:
-                    counts[b] += value[:8] + value[8:]
-                slope = value * delta
-                for axis in range(3):
-                    pulled = slope * units[axis]
-                    force[cell, axis * BINS + b] += pulled[:8] + pulled[8:]
+        for index, value in enumerate((radius, ratio, dx * inverse, dy * inverse, dz * inverse)):
+            shapes[unit, index] = value
+
+
+def add_block(values, cell, force, counts):
+    radius, ratio, *units = values
+    for chain in range(BINS // CHAIN):
+        for link in range(CHAIN):
+            b = chain * CHAIN + link
+            delta = radius - CENTRES[b] * UNIT
+            if link == 0:
+                value = jnp.exp2(LIFT - delta * delta)
+            else:
+                value = value * ratio
+            if counts is not None:
+                counts[b] += value[:8] + value[8:]
+            slope = value * delta
+            for axis in range(3):
+                pulled = slope * units[axis]
+                force[cell, axis * BINS + b] += pulled[:8] + pulled[8:]
+
+
+def add_blocks(total, row_list, cell_list, base, target, source, force, counts, spread, shapes):
+    spread_points(0, row_list, source, base, spread)
+    shape_pairs(0, cell_list, target, spread, shapes)
+    spread_points(UNROLL, row_list, source, base, spread)
+
+    def step(turn, unused):
+        at = turn * UNROLL
+        now = [[shapes[unit, index] for index in range(5)] for unit in range(UNROLL)]
+        shape_pairs(at + UNROLL, cell_list, target, spread, shapes)
+        spread_points(at + 2 * UNROLL, row_list, source, base, spread)
+        for unit in range(UNROLL):
+            add_block(now[unit], cell_list[at + unit], force, counts)
         return unused
 
-    lax.fori_loop(0, (size + (STEP_ROWS - 1)) // STEP_ROWS, step, 0)
-
-
-def pair_kernel(
-    target, points, export_count, export_cell, import_pair, import_shift,
-    from_below, from_above, from_left, from_right,
-    grad, payload, source, force, self_counts, pair_counts, meta, sems,
+    lax.fori_loop(0, (total + (UNROLL - 1)) // UNROLL, step, 0)
+
+
+def list_blocks(at, slot, cell, size, row_list, cell_list):
+    for block in range(BLOCKS):
+        row_list[at + block] = slot * BLOCKS + block
+        cell_list[at + block] = cell
+    return at + (size + (STEP_ROWS - 1)) // STEP_ROWS
+
+
+def end_list(at, slots, row_list, cell_list):
+    for spare in range(3 * UNROLL):
+        row_list[at + spare] = slots * BLOCKS
+        cell_list[at + spare] = 0
+
+
+def put_points(source, slot, first, second):
+    source[slot * POINTS : (slot + 1) * POINTS] = jnp.transpose(
+        jnp.concatenate([first, second], axis=0), (1, 0)
+    )
+
+
+def self_kernel(target, points, force, counts, source, row_list, cell_list, spread, shapes):
+    lanes = lax.broadcasted_iota(jnp.int32, (4, POINTS), 1)
+    end = 0
+    for cell in range(CELLS):
+        tile = jnp.where(lanes < points[cell], target[cell], FAR)
+        put_points(source, cell, tile, tile)
+        end = list_blocks(end, cell, cell, points[cell], row_list, cell_list)
+    end_list(end, CELLS, row_list, cell_list)
+    source[CELLS * POINTS :] = jnp.full((STEP_ROWS, 8), FAR, jnp.float32)
+    force[...] = jnp.zeros(force.shape, jnp.float32)
+    counts[...] = jnp.zeros(counts.shape, jnp.float32)
+    add_blocks(end, row_list, cell_list, 0, target, source, force, counts, spread, shapes)
+    counts[...] = 0.5 * counts[...]
+
+
+def ghost_pairs(
+    messages, neighbours, target, export_count, export_cell, import_pair, import_shift, force, counts,
+    source, import_rows, import_cells, export_rows, export_cells, meta, sems, spread, shapes,
 ):
-    lanes = lax.broadcasted_iota(jnp.int32, (4, POINTS), 1)
     rows = lax.broadcasted_iota(jnp.int32, (4, POINTS), 0)
-    messages = [
-        from_below.at[1], from_above.at[1],
-        from_left.at[0], from_left.at[1], from_left.at[2],
-        from_right.at[0], from_right.at[1], from_right.at[2],
-    ]
     copies = [
         pltpu.make_async_copy(message.at[2 * SLOTS], meta.at[index], sems.at[index])
         for index, message in enumerate(messages)
     ]
     for copy in copies:
         copy.start()
-    force[...] = jnp.zeros(force.shape, jnp.float32)
-    self_counts[...] = jnp.zeros(self_counts.shape, jnp.float32)
-    pair_counts[...] = jnp.zeros(pair_counts.shape, jnp.float32)
-
-    def put(slot, tile):
-        source[slot] = jnp.transpose(jnp.concatenate([tile, tile], axis=0), (1, 0))
-
-    for cell in range(CELLS):
-        put(cell, jnp.where(lanes < points[cell], target[cell], FAR))
-    for index, (across, along) in enumerate(NEIGHBOURS):
+    for index, (across, along) in enumerate(neighbours):
         device, inside = neighbour(across, along)
         for slot in range(SLOTS):
             shift = jnp.zeros((4, POINTS), jnp.float32)
             for axis in range(3):
                 amount = import_shift[axis * SLOTS + slot, device].astype(jnp.float32) * UNIT
                 shift = jnp.where(rows == axis, amount, shift)
-            put(CELLS + index * SLOTS + slot, messages[index][slot] + shift)
-            put(CELLS + N_JOBS + index * SLOTS + slot, messages[index][SLOTS + slot])
+            put_points(source, index * SLOTS + slot, messages[index][slot] + shift, messages[index][SLOTS + slot])
+    slots = len(neighbours) * SLOTS
+    source[slots * POINTS :] = jnp.full((STEP_ROWS, 8), FAR, jnp.float32)
     for copy in copies:
         copy.wait()
-
-    def self_job(job, unused):
-        add_pairs(job, job, job, points[job], target, source, force, self_counts)
-        return unused
-
-    lax.fori_loop(0, CELLS, self_job, 0)
-
-    for index, (across, along) in enumerate(NEIGHBOURS):
+    import_end = 0
+    export_end = 0
+    for index, (across, along) in enumerate(neighbours):
         device, inside = neighbour(across, along)
         live = jnp.where(inside, export_count[0, device], 0)
-
-        def import_job(slot, unused, index=index, device=device):
+        for slot in range(SLOTS):
+            at = index * SLOTS + slot
             size = meta[index, 0, slot].astype(jnp.int32)
-            add_pairs(
-                slot, CELLS + index * SLOTS + slot, import_pair[slot, device], size,
-                target, source, force, pair_counts,
+            import_end = list_blocks(
+                import_end, at, import_pair[slot, device], size, import_rows, import_cells
             )
-            return unused
-
-        def export_job(slot, unused, index=index, device=device, live=live):
-            size = meta[index, 0, SLOTS + slot].astype(jnp.int32)
-            add_pairs(
-                slot, CELLS + N_JOBS + index * SLOTS + slot, export_cell[slot, device], size,
-                target, source, force, None,
+            size = jnp.where(slot < live, meta[index, 0, SLOTS + slot].astype(jnp.int32), 0)
+            export_end = list_blocks(
+                export_end, at, export_cell[slot, device], size, export_rows, export_cells
             )
-            return unused
-
-        lax.fori_loop(0, SLOTS, import_job, 0)
-        lax.fori_loop(0, live, export_job, 0)
-
+    end_list(import_end, slots, import_rows, import_cells)
+    end_list(export_end, slots, export_rows, export_cells)
+    add_blocks(
+        import_end, import_rows, import_cells, 0, target, source, force, counts, spread, shapes
+    )
+    add_blocks(
+        export_end, export_rows, export_cells, 4, target, source, force, None, spread, shapes
+    )
+
+
+def near_kernel(
+    target, export_count, export_cell, import_pair, import_shift, from_below, from_above,
+    force_in, counts_in, force, counts, *scratch,
+):
+    ghost_pairs(
+        [from_below.at[1], from_above.at[1]], NEIGHBOURS[:2],
+        target, export_count, export_cell, import_pair, import_shift, force, counts, *scratch,
+    )
+
+
+def far_kernel(
+    target, points, export_count, export_cell, import_pair, import_shift, from_left, from_right,
+    force_in, counts_in, force, counts, grad, payload, *scratch,
+):
+    ghost_pairs(
+        [side.at[index] for side in (from_left, from_right) for index in range(3)], NEIGHBOURS[2:],
+        target, export_count, export_cell, import_pair, import_shift, force, counts, *scratch,
+    )
     force_scale = column(FORCE_SCALE, (BINS, POINTS))
     for cell in range(CELLS):
         for axis in range(3):
@@ -230,7 +287,7 @@
     )
     first = jnp.sum(jnp.where(bins == (low + high) % BINS, wide, 0.0), axis=0, keepdims=True)
     second = jnp.where((bins == (low + 8) % BINS) & (high == 0), wide, 0.0)
-    sums = jnp.sum(0.5 * self_counts[...] + pair_counts[...], axis=1)
+    sums = jnp.sum(counts[...], axis=1)
     sums = jnp.sum(sums, axis=1, keepdims=True) * column(COUNT_SCALE, (BINS, POINTS))
     second = second + jnp.where(lane == bins + BINS, sums, 0.0)
     total = points[0]
@@ -320,6 +377,78 @@
     return lax.ppermute(value, "sky", [(i, (i + by) % count) for i in range(count)])
 
 
+FORCE_SHAPE = (CELLS, 3 * BINS, 8, POINTS)
+COUNT_SHAPE = (BINS, 8, POINTS)
+
+
+def list_space(slots):
+    return pltpu.SMEM((slots * BLOCKS + BLOCKS + 3 * UNROLL,), jnp.int32)
+
+
+def stage_space():
+    return [
+        pltpu.VMEM((UNROLL, 3, STEP_ROWS, POINTS), jnp.float32),
+        pltpu.VMEM((UNROLL, 5, STEP_ROWS, POINTS), jnp.float32),
+    ]
+
+
+def ghost_space(messages):
+    slots = messages * SLOTS
+    return (
+        [pltpu.VMEM((slots * POINTS + STEP_ROWS, 8), jnp.float32)]
+        + [list_space(slots)] * 4
+        + [pltpu.SMEM((messages, 4, POINTS), jnp.float32), pltpu.SemaphoreType.DMA((messages,))]
+        + stage_space()
+    )
+
+
+def cost(microseconds):
+    return pl.CostEstimate(flops=0, transcendentals=0, bytes_accessed=int(microseconds * 3.0e6))
+
+
+def self_pairs(target, cell_points):
+    return pl.pallas_call(
+        self_kernel,
+        out_shape=[f32(*FORCE_SHAPE), f32(*COUNT_SHAPE)],
+        in_specs=[VMEM, SMEM],
+        out_specs=[VMEM] * 2,
+        scratch_shapes=[pltpu.VMEM((CELLS * POINTS + STEP_ROWS, 8), jnp.float32)]
+        + [list_space(CELLS)] * 2
+        + stage_space(),
+        compiler_params=PARAMS,
+        cost_estimate=cost(6),
+        name="self",
+    )(target, cell_points)
+
+
+def near_pairs(target, tables, from_below, from_above, force, counts):
+    return pl.pallas_call(
+        near_kernel,
+        out_shape=[f32(*FORCE_SHAPE), f32(*COUNT_SHAPE)],
+        in_specs=[VMEM] + [SMEM] * 4 + [VMEM] * 4,
+        out_specs=[VMEM] * 2,
+        scratch_shapes=ghost_space(2),
+        input_output_aliases={7: 0, 8: 1},
+        compiler_params=PARAMS,
+        cost_estimate=cost(4),
+        name="near",
+    )(target, *tables[1:], from_below, from_above, force, counts)
+
+
+def far_pairs(target, tables, from_left, from_right, force, counts):
+    return pl.pallas_call(
+        far_kernel,
+        out_shape=[f32(*FORCE_SHAPE), f32(*COUNT_SHAPE), f32(*GRAD_SHAPE), f32(tables[1].shape[1], 2, POINTS)],
+        in_specs=[VMEM] + [SMEM] * 5 + [VMEM] * 4,
+        out_specs=[VMEM] * 4,
+        scratch_shapes=ghost_space(6),
+        input_output_aliases={8: 0, 9: 1},
+        compiler_params=PARAMS,
+        cost_estimate=cost(12),
+        name="far",
+    )(target, *tables, from_left, from_right, force, counts)[2:]
+
+
 def body(positions, cell_points, target_log, export_count, export_cell, import_pair, import_shift):
     devices = export_count.shape[1]
     tables = (
@@ -342,24 +471,13 @@
         depth_up, depth_down, sky_up, sky_down = messages
         from_below = along_depth(depth_up, 1)
         from_above = along_depth(depth_down, -1)
+        from_below, from_above, force, counts = lax.optimization_barrier(
+            (from_below, from_above, *self_pairs(target, cell_points))
+        )
+        near = near_pairs(target, tables, from_below, from_above, force, counts)
         from_left = along_sky(jnp.stack([sky_up, from_below[2], from_above[2]]), 1)
         from_right = along_sky(jnp.stack([sky_down, from_below[0], from_above[0]]), -1)
-        grad, payload = pl.pallas_call(
-            pair_kernel,
-            out_shape=[f32(*GRAD_SHAPE), f32(devices, 2, POINTS)],
-            in_specs=[VMEM] + [SMEM] * 5 + [VMEM] * 4,
-            out_specs=[VMEM] * 2,
-            scratch_shapes=[
-                pltpu.VMEM((CELLS + 2 * N_JOBS, POINTS, 8), jnp.float32),
-                pltpu.VMEM((CELLS, 3 * BINS, 8, POINTS), jnp.float32),
-                pltpu.VMEM((BINS, 8, POINTS), jnp.float32),
-                pltpu.VMEM((BINS, 8, POINTS), jnp.float32),
-                pltpu.SMEM((8, 4, POINTS), jnp.float32),
-                pltpu.SemaphoreType.DMA((8,)),
-            ],
-            compiler_params=PARAMS,
-            name="pairs",
-        )(target, *tables, from_below, from_above, from_left, from_right)
+        grad, payload = far_pairs(target, tables, from_left, from_right, *near)
         sums = lax.all_to_all(payload, AXES, 0, 0)
         if iteration == STEPS - 1:
             return pl.pallas_call(

time: 145 us -> 109 us (0.75); the launches traced: 146 us -> 108 us
  Pallas kernels: 59.3 us -> 37.7 us
  waiting for transfers between devices: 9.43 us -> 0.02 us
  blocking collectives: 51.7 us -> 43.5 us
    pallas_call x2 -> x6, Pallas kernels: 55.4 us -> 33.7 us  [the longest x2 14.4 us: far_pairs(): pl.pallas_call(far_kernel, out_shape=[f32(*FORCE_SHAPE), f32(*COUNT_SHAPE...]
    all_to_all x2, blocking collectives: 51.7 us -> 43.5 us  [body(): sums = lax.all_to_all(payload, AXES, 0, 0)]
    ppermute x4, waiting for transfers between devices: 6.79 us -> 0.01 us  [along_depth(): lax.ppermute(value, 'depth', [(i, i + by) for i in range(count) if 0 <= i...]
    ppermute x4, waiting for transfers between devices: 2.64 us -> 0.01 us  [along_sky(): lax.ppermute(value, 'sky', [(i, (i + by) % count) for i in range(count)])]
    unnamed x11 -> x15, local copies, waits for them, and re-layouts: 2.69 us -> 4.06 us
  transfers between devices with their start and end apart: 8 -> 8, of which waited for: 4 -> 0; matrix products, arithmetic and copies ran while one was open for 0% -> 0% of each run, Pallas kernels for 0% -> 18%
where the time goes in v2:
time: 109 us; the launch traced here: 108 us
  blocking collectives  43.5 us (40%)
  Pallas kernels  37.7 us (35%)
  starting transfers between devices  21.7 us (20%)
  local copies, waits for them, and re-layouts  4.79 us (4%)
    all_to_all x2, blocking collectives, body(): sums = lax.all_to_all(payload, AXES, 0, 0)  43.5 us
    pallas_call x2, Pallas kernels, far_pairs(): pl.pallas_call(far_kernel, out_shape=[f32(*FORCE_SHAPE), f32(*COUNT_SHAPE...  14.4 us
    ppermute x4, starting transfers between devices, along_depth(): lax.ppermute(value, 'depth', [(i, i + by) for i in range(count) if 0 <= i...  11.2 us
    pallas_call x2, Pallas kernels, self_pairs(): pl.pallas_call(self_kernel, out_shape=[f32(*FORCE_SHAPE), f32(*COUNT_SHAP...  10.8 us
    ppermute x4, starting transfers between devices, along_sky(): lax.ppermute(value, 'sky', [(i, (i + by) % count) for i in range(count)])  10.5 us
    pallas_call x2, Pallas kernels, near_pairs(): pl.pallas_call(near_kernel, out_shape=[f32(*FORCE_SHAPE), f32(*COUNT_SHAP...  8.55 us
    unnamed x15, local copies, waits for them, and re-layouts  4.06 us
  transfers between devices with their start and end apart: 8, of which 0 were waited for; matrix products, arithmetic and copies ran while one was open for 0% of the time, Pallas kernels for 18%

profile of v2, /device:TPU:1, one launch (start us, length us, event | category | flops | bytes accessed | tf_op | source)
XLA Modules:
  0.0 108.0 jit_solution(464180614665621030)
XLA Ops:
  0.0 0.7 copy.22
  0.7 0.7 copy_bitcast_fusion.1
  1.4 0.7 copy-done
  2.2 0.7 copy-done.1
  2.8 0.7 copy-done.4
  3.5 1.0 first.1
  4.4 4.6 %collective-permute-start = (f32[3,7,4,128]{3,2,1,0:T(4,128)S(1)}, f32[3,7,4,128]{3,2,1,0:T(4,128)S(1)}, u32[]{:S(2)}, u32[]{:S(2)}) collective-permute-start(f32[3,7,4,128]{3,2,1,0:T(4,128)S(1)} %get-tuple-element.38), channel_id=1, source_target_pairs={{0,1},{1,2},{2,3},{3,4},{4,5},{5,6},{6,7},{8,9},{9,10},{10,11},{11... | collective-permute-start | bytes 129032 | tf_op jit(solution)/shard_map/ppermute | solution.py:372
  9.0 1.9 %collective-permute-start.1 = (f32[3,7,4,128]{3,2,1,0:T(4,128)S(1)}, f32[3,7,4,128]{3,2,1,0:T(4,128)S(1)}, u32[]{:S(2)}, u32[]{:S(2)}) collective-permute-start(f32[3,7,4,128]{3,2,1,0:T(4,128)S(1)} %get-tuple-element.39), channel_id=1, source_target_pairs={{1,0},{2,1},{3,2},{4,3},{5,4},{6,5},{7,6},{9,8},{10,9},{11,10},{12... | collective-permute-start | bytes 129032 | tf_op jit(solution)/shard_map/ppermute | solution.py:372
  11.0 0.0 copy-start.2
  11.0 0.6 copy-done.2
  11.6 5.4 %self.2 = (f32[16,48,8,128]{3,2,1,0:T(8,128)S(1)}, f32[16,8,128]{2,1,0:T(8,128)S(1)}) custom-call(f32[16,4,128]{2,1,0:T(4,128)S(1)} %get-tuple-element.36.target, s32[16]{0:T(128)S(1)} %copy-done.2), custom_call_target="tpu_custom_call" | custom-call | bytes 18000000 | tf_op jit(solution)/shard_map/self/pallas_call | solution.py:410
  17.0 0.0 collective-permute-done.from_below
  17.0 0.0 collective-permute-done.1.from_above
  17.1 2.5 %collective-permute-start.2 = (f32[3,7,4,128]{3,2,1,0:T(4,128)S(1)}, f32[3,7,4,128]{3,2,1,0:T(4,128)S(1)}, u32[]{:S(2)}, u32[]{:S(2)}) collective-permute-start(f32[3,7,4,128]{3,2,1,0:T(4,128)S(1)} %pad_maximum_fusion), channel_id=1, source_target_pairs={{0,8},{8,16},{16,24},{24,32},{32,40},{40,48},{48,56},{56,64},{64,7... | collective-permute-start | bytes 129032 | tf_op jit(solution)/shard_map/ppermute | solution.py:377
  19.6 3.1 %collective-permute-start.3 = (f32[3,7,4,128]{3,2,1,0:T(4,128)S(1)}, f32[3,7,4,128]{3,2,1,0:T(4,128)S(1)}, u32[]{:S(2)}, u32[]{:S(2)}) collective-permute-start(f32[3,7,4,128]{3,2,1,0:T(4,128)S(1)} %pad_maximum_fusion.1), channel_id=1, source_target_pairs={{0,120},{8,0},{16,8},{24,16},{32,24},{40,32},{48,40},{56,48},{64,5... | collective-permute-start | bytes 129032 | tf_op jit(solution)/shard_map/ppermute | solution.py:377
  22.7 0.7 copy-done.5
  23.3 4.3 %near.2 = (f32[16,48,8,128]{3,2,1,0:T(8,128)S(1)}, f32[16,8,128]{2,1,0:T(8,128)S(1)}) custom-call(f32[16,4,128]{2,1,0:T(4,128)S(1)} %get-tuple-element.36.target, s32[1,128]{1,0:T(1,128)S(1)} %copy-done.5, s32[3,128]{1,0:T(4,128)S(1)} %get-tuple-element.76.export_cell, ...), custom_call_target="tpu_custom_call", output_to_operand_aliasing={{0}: (7, {}), {1}: (8, {})} | custom-call | bytes 12000000 | tf_op jit(solution)/shard_map/near/pallas_call | solution.py:425
  27.7 7.2 %far.2 = (f32[16,48,8,128]{3,2,1,0:T(8,128)S(1)}, f32[16,8,128]{2,1,0:T(8,128)S(1)}, f32[16,6144]{1,0:T(8,128)S(1)}, f32[128,2,128]{2,1,0:T(2,128)S(1)}) custom-call(f32[16,4,128]{2,1,0:T(4,128)S(1)} %get-tuple-element.36.target, s32[16]{0:T(128)S(1)} %copy-done.3, s32[1,128]{1,0:T(1,128)S(1)} %copy-done.5, ...), custom_call_target="tpu_custom_call", output_to_operand_aliasing={{0}: (8, {}), {1}: (9, {})} | custom-call | bytes 36000000 | tf_op jit(solution)/shard_map/far/pallas_call | solution.py:439
  34.9 22.4 %all_to_all.10.sums = f32[128,2,128]{2,1,0:T(2,128)S(1)} all-to-all(f32[128,2,128]{2,1,0:T(2,128)S(1)} %get-tuple-element.49), channel_id=1, replica_groups=mesh['sky'=16,'depth'=8] {'sky','depth'}, dimensions={0} | all-to-all | bytes 262144 | tf_op jit(solution)/shard_map/all_to_all | solution.py:481
  57.2 1.4 %update.1 = (f32[16,4,128]{2,1,0:T(4,128)S(1)}, f32[16,4,128]{2,1,0:T(4,128)S(1)}, f32[3,7,4,128]{3,2,1,0:T(4,128)S(1)}, f32[3,7,4,128]{3,2,1,0:T(4,128)S(1)}, f...) custom-call(f32[128,2,128]{2,1,0:T(2,128)S(1)} %all_to_all.10.sums, f32[16,6144]{1,0:T(8,128)S(1)} %get-tuple-element.50.grad, ...), custom_call_target="tpu_custom_call" | custom-call | tf_op jit(solution)/shard_map/update/pallas_call | solution.py:491
  58.6 2.8 %collective-permute-start.4 = (f32[3,7,4,128]{3,2,1,0:T(4,128)S(1)}, f32[3,7,4,128]{3,2,1,0:T(4,128)S(1)}, u32[]{:S(2)}, u32[]{:S(2)}) collective-permute-start(f32[3,7,4,128]{3,2,1,0:T(4,128)S(1)} %get-tuple-element.53), channel_id=1, source_target_pairs={{0,1},{1,2},{2,3},{3,4},{4,5},{5,6},{6,7},{8,9},{9,10},{10,11},{11... | collective-permute-start | bytes 129032 | tf_op jit(solution)/shard_map/ppermute | solution.py:372
  61.4 1.9 %collective-permute-start.5 = (f32[3,7,4,128]{3,2,1,0:T(4,128)S(1)}, f32[3,7,4,128]{3,2,1,0:T(4,128)S(1)}, u32[]{:S(2)}, u32[]{:S(2)}) collective-permute-start(f32[3,7,4,128]{3,2,1,0:T(4,128)S(1)} %get-tuple-element.54), channel_id=1, source_target_pairs={{1,0},{2,1},{3,2},{4,3},{5,4},{6,5},{7,6},{9,8},{10,9},{11,10},{12... | collective-permute-start | bytes 129032 | tf_op jit(solution)/shard_map/ppermute | solution.py:372
  63.3 5.4 %self.3 = (f32[16,48,8,128]{3,2,1,0:T(8,128)S(1)}, f32[16,8,128]{2,1,0:T(8,128)S(1)}) custom-call(f32[16,4,128]{2,1,0:T(4,128)S(1)} %get-tuple-element.51.target, s32[16]{0:T(128)S(1)} %copy-done.3), custom_call_target="tpu_custom_call" | custom-call | bytes 18000000 | tf_op jit(solution)/shard_map/self/pallas_call | solution.py:410
  68.7 0.0 collective-permute-done.5.from_above
  68.8 0.9 collective-permute-start.6
  69.7 4.0 %collective-permute-start.7 = (f32[3,7,4,128]{3,2,1,0:T(4,128)S(1)}, f32[3,7,4,128]{3,2,1,0:T(4,128)S(1)}, u32[]{:S(2)}, u32[]{:S(2)}) collective-permute-start(f32[3,7,4,128]{3,2,1,0:T(4,128)S(1)} %pad_maximum_fusion.3), channel_id=1, source_target_pairs={{0,120},{8,0},{16,8},{24,16},{32,24},{40,32},{48,40},{56,48},{64,5... | collective-permute-start | bytes 129032 | tf_op jit(solution)/shard_map/ppermute | solution.py:377
  73.7 4.3 %near.3 = (f32[16,48,8,128]{3,2,1,0:T(8,128)S(1)}, f32[16,8,128]{2,1,0:T(8,128)S(1)}) custom-call(f32[16,4,128]{2,1,0:T(4,128)S(1)} %get-tuple-element.51.target, s32[1,128]{1,0:T(1,128)S(1)} %copy-done.5, s32[3,128]{1,0:T(4,128)S(1)} %get-tuple-element.76.export_cell, ...), custom_call_target="tpu_custom_call", output_to_operand_aliasing={{0}: (7, {}), {1}: (8, {})} | custom-call | bytes 12000000 | tf_op jit(solution)/shard_map/near/pallas_call | solution.py:425
  78.0 0.0 collective-permute-done.6.from_left
  78.0 0.0 collective-permute-done.7.from_right
  78.0 7.2 %far.3 = (f32[16,48,8,128]{3,2,1,0:T(8,128)S(1)}, f32[16,8,128]{2,1,0:T(8,128)S(1)}, f32[16,6144]{1,0:T(8,128)S(1)}, f32[128,2,128]{2,1,0:T(2,128)S(1)}) custom-call(f32[16,4,128]{2,1,0:T(4,128)S(1)} %get-tuple-element.51.target, s32[16]{0:T(128)S(1)} %copy-done.3, s32[1,128]{1,0:T(1,128)S(1)} %copy-done.5, ...), custom_call_target="tpu_custom_call", output_to_operand_aliasing={{0}: (8, {}), {1}: (9, {})} | custom-call | bytes 36000000 | tf_op jit(solution)/shard_map/far/pallas_call | solution.py:439
  85.3 21.2 %all_to_all.11.sums = f32[128,2,128]{2,1,0:T(2,128)S(1)} all-to-all(f32[128,2,128]{2,1,0:T(2,128)S(1)} %get-tuple-element.64), channel_id=1, replica_groups=mesh['sky'=16,'depth'=8] {'sky','depth'}, dimensions={0} | all-to-all | bytes 262144 | tf_op jit(solution)/shard_map/all_to_all | solution.py:481
  106.4 1.6 %last.1 = f32[3,16,128]{2,1,0:T(8,128)} custom-call(f32[128,2,128]{2,1,0:T(2,128)S(1)} %all_to_all.11.sums, f32[16,6144]{1,0:T(8,128)S(1)} %get-tuple-element.65.grad, f32[16,4,128]{2,1,0:T(4,128)S(1)} %get-tuple-element.66.travel, f32[16]{0:T(128)S(1)} %copy-done.6), custom_call_target="tpu_custom_call" | custom-call | tf_op jit(solution)/shard_map/last/pallas_call | solution.py:483
  (20 shorter events, 0.1 us)
Async XLA Ops:
  0.0 27.7 %copy-start.3 = (s32[16]{0:T(128)S(1)}, s32[16]{0:T(128)}, u32[]{:S(2)}) copy-start(s32[16]{0:T(128)} %points.11) | copy-start | bytes 196
  1.4 0.7 copy-start
  2.2 0.7 copy-start.1
  2.8 0.7 copy-start.4
  4.4 12.6 %collective-permute-start = (f32[3,7,4,128]{3,2,1,0:T(4,128)S(1)}, f32[3,7,4,128]{3,2,1,0:T(4,128)S(1)}, u32[]{:S(2)}, u32[]{:S(2)}) collective-permute-start(f32[3,7,4,128]{3,2,1,0:T(4,128)S(1)} %get-tuple-element.38), channel_id=1, source_target_pairs={{0,1},{1,2},{2,3},{3,4},{4,5},{5,6},{6,7},{8,9},{9,10},{10,11},{11... | collective-permute-start | bytes 129032 | tf_op jit(solution)/shard_map/ppermute | solution.py:372
  9.0 8.0 %collective-permute-start.1 = (f32[3,7,4,128]{3,2,1,0:T(4,128)S(1)}, f32[3,7,4,128]{3,2,1,0:T(4,128)S(1)}, u32[]{:S(2)}, u32[]{:S(2)}) collective-permute-start(f32[3,7,4,128]{3,2,1,0:T(4,128)S(1)} %get-tuple-element.39), channel_id=1, source_target_pairs={{1,0},{2,1},{3,2},{4,3},{5,4},{6,5},{7,6},{9,8},{10,9},{11,10},{12... | collective-permute-start | bytes 129032 | tf_op jit(solution)/shard_map/ppermute | solution.py:372
  11.0 0.7 copy-start.2
  17.1 10.5 %collective-permute-start.2 = (f32[3,7,4,128]{3,2,1,0:T(4,128)S(1)}, f32[3,7,4,128]{3,2,1,0:T(4,128)S(1)}, u32[]{:S(2)}, u32[]{:S(2)}) collective-permute-start(f32[3,7,4,128]{3,2,1,0:T(4,128)S(1)} %pad_maximum_fusion), channel_id=1, source_target_pairs={{0,8},{8,16},{16,24},{24,32},{32,40},{40,48},{48,56},{56,64},{64,7... | collective-permute-start | bytes 129032 | tf_op jit(solution)/shard_map/ppermute | solution.py:377
  19.6 8.0 %collective-permute-start.3 = (f32[3,7,4,128]{3,2,1,0:T(4,128)S(1)}, f32[3,7,4,128]{3,2,1,0:T(4,128)S(1)}, u32[]{:S(2)}, u32[]{:S(2)}) collective-permute-start(f32[3,7,4,128]{3,2,1,0:T(4,128)S(1)} %pad_maximum_fusion.1), channel_id=1, source_target_pairs={{0,120},{8,0},{16,8},{24,16},{32,24},{40,32},{48,40},{56,48},{64,5... | collective-permute-start | bytes 129032 | tf_op jit(solution)/shard_map/ppermute | solution.py:377
  22.7 0.7 copy-start.5
  23.3 33.9 %copy-start.6 = (f32[16]{0:T(128)S(1)}, f32[16]{0:T(128)}, u32[]{:S(2)}) copy-start(f32[16]{0:T(128)} %target_log.3) | copy-start | bytes 196
  58.6 10.1 %collective-permute-start.4 = (f32[3,7,4,128]{3,2,1,0:T(4,128)S(1)}, f32[3,7,4,128]{3,2,1,0:T(4,128)S(1)}, u32[]{:S(2)}, u32[]{:S(2)}) collective-permute-start(f32[3,7,4,128]{3,2,1,0:T(4,128)S(1)} %get-tuple-element.53), channel_id=1, source_target_pairs={{0,1},{1,2},{2,3},{3,4},{4,5},{5,6},{6,7},{8,9},{9,10},{10,11},{11... | collective-permute-start | bytes 129032 | tf_op jit(solution)/shard_map/ppermute | solution.py:372
  61.4 7.3 %collective-permute-start.5 = (f32[3,7,4,128]{3,2,1,0:T(4,128)S(1)}, f32[3,7,4,128]{3,2,1,0:T(4,128)S(1)}, u32[]{:S(2)}, u32[]{:S(2)}) collective-permute-start(f32[3,7,4,128]{3,2,1,0:T(4,128)S(1)} %get-tuple-element.54), channel_id=1, source_target_pairs={{1,0},{2,1},{3,2},{4,3},{5,4},{6,5},{7,6},{9,8},{10,9},{11,10},{12... | collective-permute-start | bytes 129032 | tf_op jit(solution)/shard_map/ppermute | solution.py:372
  68.8 9.2 %collective-permute-start.6 = (f32[3,7,4,128]{3,2,1,0:T(4,128)S(1)}, f32[3,7,4,128]{3,2,1,0:T(4,128)S(1)}, u32[]{:S(2)}, u32[]{:S(2)}) collective-permute-start(f32[3,7,4,128]{3,2,1,0:T(4,128)S(1)} %pad_maximum_fusion.2), channel_id=1, source_target_pairs={{0,8},{8,16},{16,24},{24,32},{32,40},{40,48},{48,56},{56,64},{64,7... | collective-permute-start | bytes 129032 | tf_op jit(solution)/shard_map/ppermute | solution.py:377
  69.7 8.3 %collective-permute-start.7 = (f32[3,7,4,128]{3,2,1,0:T(4,128)S(1)}, f32[3,7,4,128]{3,2,1,0:T(4,128)S(1)}, u32[]{:S(2)}, u32[]{:S(2)}) collective-permute-start(f32[3,7,4,128]{3,2,1,0:T(4,128)S(1)} %pad_maximum_fusion.3), channel_id=1, source_target_pairs={{0,120},{8,0},{16,8},{24,16},{32,24},{40,32},{48,40},{56,48},{64,5... | collective-permute-start | bytes 129032 | tf_op jit(solution)/shard_map/ppermute | solution.py:377
